TPU v7x, 32 devices: a whole 2x2x4 slice. The times are simulated.
32 devices in a mesh: tm: 8 (over y, x, core), rows: 4 (over z).
Axes of the slice: x: 2, y: 2, z: 4, core: 2. Of those that a mesh axis runs over, the one named last changes fastest.
Arguments:
- starts: float32 [8, 2, 32, 8192], P('tm', None, 'rows'), may hold values from -6 to 6
- conductivity: float32 [32, 8192], P('rows'), may hold values from 0.03 to 0.12
Outputs:
- new_ends: float32 [8, 2, 32, 8192], P('tm', None, 'rows')
- coarse_next: float32 [8, 2, 4, 1024], P('tm')
All inputs are finite; a program needn't handle non-finite values.
Results may differ from a plain program's by a relative error of at most 0.0001.
Values sent between devices are 32-bit elements; how exact they have to be, the bound alone decides.
A program may use at most 64 MiB of HBM per device.

v0:
```python
import functools
import math

import jax
import jax.numpy as jnp
from jax import lax
from jax.experimental import pallas as pl
from jax.experimental.pallas import tpu as pltpu
from jax.sharding import PartitionSpec as P

FINE = 8
COARSE = 2
COARSEN = 8
EXCHANGE = 0.05
TRACER_DIFF = 0.5

SUB = 8
LANES = 128
MESH = pl.DeviceIdType.MESH
SHARE = 4


def roll_left(v):
    width = v.shape[1]
    r = pltpu.roll(v, width - 1, 1)
    last = r[:, width - LANES:]
    lane = lax.broadcasted_iota(jnp.int32, last.shape, 1)
    last = jnp.where(lane == LANES - 1, pltpu.roll(last, SUB - 1, 0), last)
    if width == LANES:
        return last
    return jnp.concatenate([r[:, : width - LANES], last], axis=1)


def roll_right(v):
    width = v.shape[1]
    r = pltpu.roll(v, 1, 1)
    first = r[:, :LANES]
    lane = lax.broadcasted_iota(jnp.int32, first.shape, 1)
    first = jnp.where(lane == 0, pltpu.roll(first, 1, 0), first)
    if width == LANES:
        return first
    return jnp.concatenate([first, r[:, LANES:]], axis=1)


def exact_dot(x, w):
    rows = x.shape[0]
    hi = x.astype(jnp.bfloat16)
    rest = x - hi.astype(jnp.float32)
    mid = rest.astype(jnp.bfloat16)
    low = (rest - mid.astype(jnp.float32)).astype(jnp.bfloat16)
    y = jnp.dot(jnp.concatenate([hi.astype(jnp.float32), mid.astype(jnp.float32), low.astype(jnp.float32)], axis=0).astype(jnp.bfloat16), w,
                preferred_element_type=jnp.float32)
    return y[:rows] + y[rows:2 * rows] + y[2 * rows:]


def neighbours(v, above, below, k_up, k_down, k_left, k_right):
    return (k_right * roll_left(v) + k_left * roll_right(v)) + (k_down * below + k_up * above)


def kernel(nt, nr, group, s_hbm, k_hbm, out_ref, nxt_ref,
           s_ref, k_ref, in_sem, vb, own, kown, kh, kr, kl, kd, ku, ch, ct, pool, kcs, rss, rfs, kc, rsn, rf, jall,
           vsend, vrecv, ksend, krecv, kfwd, kcsend, kcrecv, rssend, rsrecv, rfsend, rfrecv, jsend, jrecv, tok_down, tok_up):
    t = lax.axis_index("tm")
    r = lax.axis_index("rows")
    width = own.shape[-1]
    tiles = width // LANES
    member = lax.rem(t, group)
    base = t - member
    has_up = r > 0
    has_down = r < nr - 1
    has_prev = t > 0
    has_next = t < nt - 1

    k_in = pltpu.make_async_copy(k_hbm, k_ref, in_sem.at[0])
    s_in = pltpu.make_async_copy(s_hbm, s_ref, in_sem.at[1])
    k_in.start()
    s_in.start()

    barrier = pltpu.get_barrier_semaphore()

    def greet(tm, row):
        pl.semaphore_signal(barrier, inc=1, device_id=(tm, row), device_id_type=MESH)

    pl.when(has_up)(lambda: greet(t, r - 1))
    pl.when(has_down)(lambda: greet(t, r + 1))
    for o in range(1, nt):
        greet(lax.rem(t + o, nt), r)

    cell = lax.broadcasted_iota(jnp.int32, pool.shape, 0)
    block = lax.broadcasted_iota(jnp.int32, pool.shape, 1)
    inside = (cell >= block * COARSEN) & (cell < (block + 1) * COARSEN)
    pool[...] = jnp.where(inside, 1.0 / (COARSEN * COARSEN), 0.0).astype(jnp.bfloat16)
    k_in.wait()
    s_in.wait()

    def split_row(ref, row):
        return jnp.concatenate(
            [ref[pl.ds(m * SUB + row, SUB, stride=tiles * SUB), :] for m in range(tiles)], axis=1)

    sums = [None, None, None]
    for row in range(SUB):
        for f in range(2):
            x = split_row(s_ref.at[f], row)
            own[row, f] = x
            vb[0, SUB + row, f] = x
            sums[f] = x if sums[f] is None else sums[f] + x
        x = split_row(k_ref, row)
        kown[row] = x
        sums[2] = x if sums[2] is None else sums[2] + x

    coarse = exact_dot(jnp.concatenate(sums, axis=0), pool[...])
    rss[0] = coarse[:SUB]
    rss[1] = coarse[SUB:2 * SUB]
    kcs[...] = coarse[2 * SUB:]
    kc[r] = coarse[2 * SUB:]

    @pl.when(jnp.logical_not(has_up))
    def _():
        vb[0, 0:SUB] = jnp.zeros((SUB,) + vb.shape[2:], jnp.float32)
        kh[0] = jnp.zeros(kh.shape[1:], jnp.float32)

    @pl.when(jnp.logical_not(has_down))
    def _():
        vb[0, 2 * SUB:] = jnp.zeros((SUB,) + vb.shape[2:], jnp.float32)
        kh[1] = jnp.zeros(kh.shape[1:], jnp.float32)

    pl.semaphore_wait(barrier, (nt - 1) + has_up.astype(jnp.int32) + has_down.astype(jnp.int32))

    def tell(tok, row):
        pl.semaphore_signal(tok, inc=1, device_id=(t, row), device_id_type=MESH)

    pl.when(jnp.logical_not(has_up) & has_down)(lambda: tell(tok_down, r + 1))
    pl.when(jnp.logical_not(has_down) & has_up)(lambda: tell(tok_up, r - 1))

    def v_copy(side, d):
        if side == 0:
            return pltpu.make_async_remote_copy(
                own.at[SUB - d], vb.at[0, SUB - d], vsend.at[side, d - 1], vrecv.at[side, d - 1],
                device_id=(t, r + 1), device_id_type=MESH)
        return pltpu.make_async_remote_copy(
            own.at[d - 1], vb.at[0, 2 * SUB - 1 + d], vsend.at[side, d - 1], vrecv.at[side, d - 1],
            device_id=(t, r - 1), device_id_type=MESH)

    def k_copy(side, d):
        return pltpu.make_async_remote_copy(
            kown.at[SUB - d if side == 0 else d - 1], kh.at[side, d - 1], ksend.at[side, d - 1], krecv.at[side, d - 1],
            device_id=(t, r + 1 if side == 0 else r - 1), device_id_type=MESH)

    def k_forward(side, d, o):
        return pltpu.make_async_remote_copy(
            kh.at[side, d - 1], kh.at[side, d - 1], kfwd.at[side, d - 1, o], krecv.at[side, d - 1],
            device_id=(base + lax.rem(member + o, group), r), device_id_type=MESH)

    def when_mine(d, cond, act):
        pl.when(cond & (member == (d - 1) % group))(act)

    sends = (has_down, has_up)
    gets = (has_up, has_down)
    for d in range(1, FINE + 1):
        for side in range(2):
            when_mine(d, sends[side], lambda: k_copy(side, d).start())
    for side in range(2):
        @pl.when(sends[side])
        def _():
            v_copy(side, 1).start()
    for d in range(2, FINE + 1):
        for side in range(2):
            @pl.when(sends[side])
            def _():
                v_copy(side, d).start()

    def kc_copy(o):
        return pltpu.make_async_remote_copy(
            kcs, kc.at[r], kcsend.at[o], kcrecv.at[o],
            device_id=(t, lax.rem(r + o, nr)), device_id_type=MESH)

    def rs_first():
        return pltpu.make_async_remote_copy(
            rss, rsn.at[r], rssend.at[0], rsrecv.at[0],
            device_id=(t - 1, r), device_id_type=MESH)

    def rs_copy(o):
        return pltpu.make_async_remote_copy(
            rsn.at[r], rsn.at[r], rssend.at[o], rsrecv.at[o],
            device_id=(t, lax.rem(r + o, nr)), device_id_type=MESH)

    pl.when(has_prev)(lambda: rs_first().start())

    @pl.when(has_up)
    def _():
        pl.semaphore_wait(tok_down, 1)
        pl.when(has_down)(lambda: tell(tok_down, r + 1))

    def columns_of(i, k):
        kr[i] = 0.5 * (k + roll_left(k))
        kl[i] = 0.5 * (k + roll_right(k))

    def centre_of(i):
        total = (kr[i] + kl[i]) + (ku[i] + kd[i])
        ch[i] = (1.0 - EXCHANGE) - total
        ct[i] = (1.0 - EXCHANGE) - TRACER_DIFF * total

    for row in range(SUB):
        k = kown[row]
        columns_of(SUB + row, k)
        if row < SUB - 1:
            face = 0.5 * (k + kown[row + 1])
            kd[SUB + row] = face
            ku[SUB + row + 1] = face
        if 0 < row < SUB - 1:
            centre_of(SUB + row)

    @pl.when(has_down)
    def _():
        pl.semaphore_wait(tok_up, 1)
        pl.when(has_up)(lambda: tell(tok_up, r - 1))

    for o in range(1, nr):
        kc_copy(o).start()

    def row_pair(level, diagonal):
        p = lax.rem(level + 1, 2)
        new = []
        for i in (SUB + level - diagonal, 2 * SUB - 1 - level + diagonal):
            faces = ku[i], kd[i], kl[i], kr[i]
            heat, tracer = vb[p, i, 0], vb[p, i, 1]
            around_h = neighbours(heat, vb[p, i - 1, 0], vb[p, i + 1, 0], *faces)
            around_t = neighbours(tracer, vb[p, i - 1, 1], vb[p, i + 1, 1], *faces)
            new.append((i, (ch[i] * heat + EXCHANGE * tracer) + around_h,
                        (ct[i] * tracer + EXCHANGE * heat) + TRACER_DIFF * around_t))
        for i, heat, tracer in new:
            vb[1 - p, i, 0] = heat
            vb[1 - p, i, 1] = tracer

    def run_diagonal(diagonal):
        def step(level, carry):
            row_pair(level, diagonal)
            return carry
        lax.fori_loop(1, min(FINE, SUB // 2 - 1 + diagonal) + 1, step, 0)

    for diagonal in range(2 - SUB // 2, 1):
        run_diagonal(diagonal)

    for d in range(1, FINE + 1):
        for side in range(2):
            def pass_on():
                k_copy(side, d).wait_recv()
                for o in range(1, group):
                    k_forward(side, d, o).start()
            when_mine(d, gets[side], pass_on)

    outside = (jnp.where(has_up, 1.0, 0.0), jnp.where(has_down, 1.0, 0.0))
    for d in range(1, FINE + 1):
        for side in range(2):
            @pl.when(gets[side])
            def _():
                v_copy(side, d).wait_recv()

            pl.when(gets[side] & (member != (d - 1) % group))(lambda: k_copy(side, d).wait_recv())
            k = kh[side, d - 1]
            if d > 1:
                inner = kh[side, d - 2]
            else:
                inner = kown[0 if side == 0 else SUB - 1]
            face = 0.5 * (k + inner)
            edge = face * outside[side] if d == 1 else face
            i = SUB - d if side == 0 else 2 * SUB - 1 + d
            columns_of(i, k)
            if side == 0:
                ku[i + 1] = face
                kd[i] = edge
                centre_of(i + 1)
            else:
                kd[i - 1] = face
                ku[i] = edge
                centre_of(i - 1)
        run_diagonal(d)
        if d == FINE // 2:
            @pl.when(has_next)
            def _():
                rs_first().wait_recv()
                for o in range(1, nr):
                    rs_copy(o).start()

    ends = []
    for f in range(2):
        total = vb[0, SUB, f]
        for row in range(1, SUB):
            total = total + vb[0, SUB + row, f]
        ends.append(total)
    coarse_end = exact_dot(jnp.concatenate(ends, axis=0), pool[...])
    for f in range(2):
        rfs[f] = coarse_end[f * SUB:(f + 1) * SUB]
        rf[r, f] = coarse_end[f * SUB:(f + 1) * SUB]

    def rf_copy(o):
        return pltpu.make_async_remote_copy(
            rfs, rf.at[r], rfsend.at[o], rfrecv.at[o],
            device_id=(t, lax.rem(r + o, nr)), device_id_type=MESH)

    for o in range(1, nr):
        rf_copy(o).start()
    for o in range(1, nr):
        kc_copy(o).wait_recv()

    ratio = (FINE / COARSE) / float(COARSEN * COARSEN)
    kcv = [kc[i] for i in range(nr)]
    c_right = [ratio * 0.5 * (k + roll_left(k)) for k in kcv]
    c_left = [ratio * 0.5 * (k + roll_right(k)) for k in kcv]
    c_face = [ratio * 0.5 * kcv[0]]
    c_face += [ratio * 0.5 * (kcv[i] + kcv[i + 1]) for i in range(nr - 1)]
    c_face += [ratio * 0.5 * kcv[nr - 1]]

    rate = EXCHANGE * (FINE / COARSE)
    totals = [(c_right[i] + c_left[i]) + (c_face[i] + c_face[i + 1]) for i in range(nr)]
    c_centre = [[(1.0 - rate) - x for x in totals], [(1.0 - rate) - TRACER_DIFF * x for x in totals]]

    def coarse_prop(state):
        for substep in range(COARSE):
            new = []
            for f in range(2):
                rows = state[f * nr:(f + 1) * nr]
                other = state[(1 - f) * nr:(2 - f) * nr]
                for i in range(nr):
                    v = rows[i]
                    around = c_right[i] * roll_left(v) + c_left[i] * roll_right(v)
                    rowwise = None
                    if i > 0:
                        rowwise = c_face[i] * rows[i - 1]
                    if i < nr - 1:
                        below = c_face[i + 1] * rows[i + 1]
                        rowwise = below if rowwise is None else rowwise + below
                    if rowwise is not None:
                        around = around + rowwise
                    if f == 1:
                        around = TRACER_DIFF * around
                    new.append((c_centre[f][i] * v + rate * other[i]) + around)
            state = tuple(new)
        return state

    for o in range(1, nr):
        rf_copy(o).wait_recv()

    def j_copy(o):
        return pltpu.make_async_remote_copy(
            jall.at[t], jall.at[t], jsend.at[o], jrecv.at[t],
            device_id=(t + o, r), device_id_type=MESH)

    @pl.when(has_next)
    def _():
        for o in range(1, nr):
            rs_copy(o).wait_recv()
        jall[t] = rf[...] - rsn[...]

    for o in range(1, nt):
        pl.when(t + o < nt)(lambda: j_copy(o).start())

    def link(n, state):
        pltpu.make_async_remote_copy(
            jall.at[n], jall.at[n], jsend.at[0], jrecv.at[n],
            device_id=(n, r), device_id_type=MESH).wait_recv()
        state = coarse_prop(state)
        return tuple(state[f * nr + i] + jall[n, i, f] for f in range(2) for i in range(nr))

    state = tuple(jnp.zeros((SUB, width // COARSEN), jnp.float32) for _ in range(2 * nr))
    state = lax.fori_loop(0, t, link, state)
    state = coarse_prop(state)

    mine = [state[f * nr] for f in range(2)]
    for f in range(2):
        for i in range(nr):
            value = state[f * nr + i]
            nxt_ref[f, pl.ds(i, SUB, stride=nr), :] = value + rf[i, f]
            if i > 0:
                mine[f] = jnp.where(r == i, value, mine[f])

    spread_back = lax.dot_general(
        *split_terms(jnp.concatenate(mine, axis=0), pool), (((1,), (1,)), ((), ())),
        preferred_element_type=jnp.float32) * float(COARSEN * COARSEN)
    rows = 2 * SUB
    fix = spread_back[:rows] + spread_back[rows:2 * rows] + spread_back[2 * rows:]
    for f in range(2):
        for row in range(SUB):
            end = vb[0, SUB + row, f] + fix[f * SUB:(f + 1) * SUB]
            for m in range(tiles):
                out_ref[f, pl.ds(m * SUB + row, SUB, stride=tiles * SUB), :] = end[:, m * LANES:(m + 1) * LANES]

    for d in range(1, FINE + 1):
        for side in range(2):
            pl.when(sends[side])(lambda: v_copy(side, d).wait_send())
            when_mine(d, sends[side], lambda: k_copy(side, d).wait_send())

            def passed_on():
                for o in range(1, group):
                    k_forward(side, d, o).wait_send()
            when_mine(d, gets[side], passed_on)
    for o in range(1, nr):
        kc_copy(o).wait_send()
        rf_copy(o).wait_send()

    pl.when(has_prev)(lambda: rs_first().wait_send())

    @pl.when(has_next)
    def _():
        for o in range(1, nr):
            rs_copy(o).wait_send()

    for o in range(1, nt):
        pl.when(t + o < nt)(lambda: j_copy(o).wait_send())


def split_terms(x, pool):
    hi = x.astype(jnp.bfloat16).astype(jnp.float32)
    mid = (x - hi).astype(jnp.bfloat16).astype(jnp.float32)
    low = x - hi - mid
    return jnp.concatenate([hi, mid, low], axis=0).astype(jnp.bfloat16), pool[...]


def body(nt, nr, starts, conductivity):
    rows, columns = conductivity.shape
    assert rows == SUB == COARSEN == FINE
    width = columns // SUB
    blocks = columns // LANES
    ncoarse = width // COARSEN
    group = math.gcd(SHARE, nt)
    slab = starts[0].reshape(2, rows, blocks, LANES).transpose(0, 2, 1, 3).reshape(2, blocks * rows, LANES)
    kappa = conductivity.reshape(rows, blocks, LANES).transpose(1, 0, 2).reshape(blocks * rows, LANES)
    f32 = jnp.float32
    dma = pltpu.SemaphoreType.DMA
    ends, following = pl.pallas_call(
        functools.partial(kernel, nt, nr, group),
        out_shape=(
            jax.ShapeDtypeStruct((2, blocks * rows, LANES), f32),
            jax.ShapeDtypeStruct((2, SUB * nr, ncoarse), f32),
        ),
        in_specs=[pl.BlockSpec(memory_space=pltpu.HBM)] * 2,
        out_specs=[pl.BlockSpec(memory_space=pltpu.VMEM)] * 2,
        scratch_shapes=[
            pltpu.VMEM((2, blocks * rows, LANES), f32),
            pltpu.VMEM((blocks * rows, LANES), f32),
            dma((2,)),
            pltpu.VMEM((2, 3 * SUB, 2, SUB, width), f32),
            pltpu.VMEM((SUB, 2, SUB, width), f32),
            pltpu.VMEM((SUB, SUB, width), f32),
            pltpu.VMEM((2, FINE, SUB, width), f32),
            pltpu.VMEM((3 * SUB, SUB, width), f32),
            pltpu.VMEM((3 * SUB, SUB, width), f32),
            pltpu.VMEM((3 * SUB, SUB, width), f32),
            pltpu.VMEM((3 * SUB, SUB, width), f32),
            pltpu.VMEM((3 * SUB, SUB, width), f32),
            pltpu.VMEM((3 * SUB, SUB, width), f32),
            pltpu.VMEM((width, ncoarse), jnp.bfloat16),
            pltpu.VMEM((SUB, ncoarse), f32),
            pltpu.VMEM((2, SUB, ncoarse), f32),
            pltpu.VMEM((2, SUB, ncoarse), f32),
            pltpu.VMEM((nr, SUB, ncoarse), f32),
            pltpu.VMEM((nr, 2, SUB, ncoarse), f32),
            pltpu.VMEM((nr, 2, SUB, ncoarse), f32),
            pltpu.VMEM((nt, nr, 2, SUB, ncoarse), f32),
            dma((2, FINE)), dma((2, FINE)),
            dma((2, FINE)), dma((2, FINE)), dma((2, FINE, group)),
            dma((nr,)), dma((nr,)),
            dma((nr,)), dma((nr,)),
            dma((nr,)), dma((nr,)),
            dma((nt,)), dma((nt,)),
            pltpu.SemaphoreType.REGULAR, pltpu.SemaphoreType.REGULAR,
        ],
        compiler_params=pltpu.CompilerParams(
            collective_id=0, has_side_effects=True, vmem_limit_bytes=48 * 1024 * 1024),
        name="parareal",
    )(slab, kappa)
    new_ends = ends.reshape(2, blocks, rows, LANES).transpose(0, 2, 1, 3).reshape(2, rows, columns)
    coarse_next = following.reshape(2, SUB, nr, ncoarse).transpose(0, 2, 1, 3).reshape(2, nr, SUB * ncoarse)
    return new_ends[None], coarse_next[None]


def solution(mesh):
    nt, nr = mesh.shape["tm"], mesh.shape["rows"]
    in_specs = (P("tm", None, "rows", None), P("rows", None))
    out_specs = (P("tm", None, "rows", None), P("tm", None, None, None))
    return jax.shard_map(functools.partial(body, nt, nr), mesh=mesh, in_specs=in_specs, out_specs=out_specs, check_vma=False)
```

profile of v0, /device:TPU:5, one launch (start us, length us, event | category | flops | bytes accessed | tf_op | source)
XLA Modules:
  0.0 35.0 jit_solution(10458822044103163819)
XLA Ops:
  0.6 0.0 copy-start
  0.6 1.0 %copy-done = f32[1,2,8,8192]{3,2,1,0:T(8,128)S(1)} copy-done((f32[1,2,8,8192]{3,2,1,0:T(8,128)S(1)}, f32[1,2,8,8192]{3,2,1,0:T(8,128)}, u32[]{:S(2)}) %copy-start) | copy-done | bytes 524312
  1.7 0.0 copy-start.1
  1.7 0.9 %copy-done.1 = f32[8,8192]{1,0:T(8,128)S(1)} copy-done((f32[8,8192]{1,0:T(8,128)S(1)}, f32[8,8192]{1,0:T(8,128)}, u32[]{:S(2)}) %copy-start.1) | copy-done | bytes 262168
  2.6 30.9 %parareal.1 = (f32[2,512,128]{2,1,0:T(8,128)S(1)}, f32[2,32,128]{2,1,0:T(8,128)S(1)}) custom-call(f32[2,512,128]{2,1,0:T(8,128)S(1)} %bitcast.20, f32[512,128]{1,0:T(8,128)S(1)} %bitcast.22), custom_call_target="tpu_custom_call" | custom-call | tf_op jit(solution)/shard_map/parareal/pallas_call | solution.py:430
  33.6 0.8 %copy.7 = f32[1,2,8,8192]{3,2,1,0:T(8,128)} copy(f32[1,2,8,8192]{3,2,1,0:T(8,128)S(1)} %bitcast.21) | data formatting | bytes 1048576
  34.4 0.6 %copy.8 = f32[1,2,4,1024]{3,2,1,0:T(4,128)} copy(f32[1,2,4,1024]{3,2,1,0:T(4,128)S(1)} %bitcast.23) | data formatting | bytes 65536
Async XLA Ops:
  0.6 1.0 %copy-start = (f32[1,2,8,8192]{3,2,1,0:T(8,128)S(1)}, f32[1,2,8,8192]{3,2,1,0:T(8,128)}, u32[]{:S(2)}) copy-start(f32[1,2,8,8192]{3,2,1,0:T(8,128)} %param.2) | copy-start | bytes 1572868
  1.7 0.9 %copy-start.1 = (f32[8,8192]{1,0:T(8,128)S(1)}, f32[8,8192]{1,0:T(8,128)}, u32[]{:S(2)}) copy-start(f32[8,8192]{1,0:T(8,128)} %param.3) | copy-start | bytes 786436
where the time goes:
time: 35.2 us; the launch traced here: 35 us
  Pallas kernels  30.9 us (88%)
  local copies, waits for them, and re-layouts  3.39 us (10%)
  between operations  0.65 us (2%)
    pallas_call x1, Pallas kernels, body(): pl.pallas_call(functools.partial(kernel, nt, nr, group), out_shape=(jax.S...  30.9 us
    unnamed x6, local copies, waits for them, and re-layouts  3.39 us

commit v1 on v0

--- a/solution.py
+++ b/solution.py
@@ -416,6 +416,15 @@
     return jnp.concatenate([hi, mid, low], axis=0).astype(jnp.bfloat16), pool[...]
 
 
+def deliver(ends, following, ends_out, following_out, sem):
+    first = pltpu.make_async_copy(ends, ends_out, sem.at[0])
+    second = pltpu.make_async_copy(following, following_out, sem.at[1])
+    first.start()
+    second.start()
+    first.wait()
+    second.wait()
+
+
 def body(nt, nr, starts, conductivity):
     rows, columns = conductivity.shape
     assert rows == SUB == COARSEN == FINE
@@ -425,6 +434,8 @@
     group = math.gcd(SHARE, nt)
     slab = starts[0].reshape(2, rows, blocks, LANES).transpose(0, 2, 1, 3).reshape(2, blocks * rows, LANES)
     kappa = conductivity.reshape(rows, blocks, LANES).transpose(1, 0, 2).reshape(blocks * rows, LANES)
+    slab = pltpu.with_memory_space_constraint(slab, pltpu.HBM)
+    kappa = pltpu.with_memory_space_constraint(kappa, pltpu.HBM)
     f32 = jnp.float32
     dma = pltpu.SemaphoreType.DMA
     ends, following = pl.pallas_call(
@@ -469,6 +480,18 @@
             collective_id=0, has_side_effects=True, vmem_limit_bytes=48 * 1024 * 1024),
         name="parareal",
     )(slab, kappa)
+    ends, following = pl.pallas_call(
+        deliver,
+        out_shape=(
+            jax.ShapeDtypeStruct(ends.shape, f32),
+            jax.ShapeDtypeStruct(following.shape, f32),
+        ),
+        in_specs=[pl.BlockSpec(memory_space=pltpu.VMEM)] * 2,
+        out_specs=[pl.BlockSpec(memory_space=pltpu.HBM)] * 2,
+        scratch_shapes=[dma((2,))],
+        compiler_params=pltpu.CompilerParams(vmem_limit_bytes=1024 * 1024),
+        name="deliver",
+    )(ends, following)
     new_ends = ends.reshape(2, blocks, rows, LANES).transpose(0, 2, 1, 3).reshape(2, rows, columns)
     coarse_next = following.reshape(2, SUB, nr, ncoarse).transpose(0, 2, 1, 3).reshape(2, nr, SUB * ncoarse)
     return new_ends[None], coarse_next[None]

time: 35.2 us -> 32.5 us (0.923)
  local copies, waits for them, and re-layouts: 3.39 us -> 0 us
  Pallas kernels: 30.9 us -> 31.8 us
    unnamed x6 -> x0, local copies, waits for them, and re-layouts: 3.39 us -> none
    pallas_call x0 -> x1, Pallas kernels: none -> 0.81 us  [body(): pl.pallas_call(deliver, out_shape=(jax.ShapeDtypeStruct(ends.shape, f32),...]
where the time goes in v1:
time: 32.5 us; the launch traced here: 32.4 us
  Pallas kernels  31.8 us (98%)
  between operations  0.64 us (2%)
    pallas_call x1, Pallas kernels, body(): pl.pallas_call(functools.partial(kernel, nt, nr, group), out_shape=(jax.S...  30.9 us
    pallas_call x1, Pallas kernels, body(): pl.pallas_call(deliver, out_shape=(jax.ShapeDtypeStruct(ends.shape, f32),...  0.81 us

profile of v1, /device:TPU:5, one launch (start us, length us, event | category | flops | bytes accessed | tf_op | source)
XLA Modules:
  0.0 32.4 jit_solution(17465424926807683591)
XLA Ops:
  0.6 30.9 %parareal.1 = (f32[2,512,128]{2,1,0:T(8,128)S(1)}, f32[2,32,128]{2,1,0:T(8,128)S(1)}) custom-call(f32[2,512,128]{2,1,0:T(8,128)} %bitcast.20, f32[512,128]{1,0:T(8,128)} %bitcast.21), custom_call_target="tpu_custom_call" | custom-call | tf_op jit(solution)/shard_map/parareal/pallas_call | solution.py:441
  31.6 0.8 %deliver.1 = (f32[2,512,128]{2,1,0:T(8,128)}, f32[2,32,128]{2,1,0:T(8,128)}) custom-call(f32[2,512,128]{2,1,0:T(8,128)S(1)} %get-tuple-element.6.ends, f32[2,32,128]{2,1,0:T(8,128)S(1)} %get-tuple-element.7.following), custom_call_target="tpu_custom_call" | custom-call | tf_op jit(solution)/shard_map/deliver/pallas_call | solution.py:483

commit v2 on v1

v2 whole, which is shorter than its diff:
```python
import functools
import math

import jax
import jax.numpy as jnp
from jax import lax
from jax.experimental import pallas as pl
from jax.experimental.pallas import tpu as pltpu
from jax.sharding import PartitionSpec as P

FINE = 8
COARSE = 2
COARSEN = 8
EXCHANGE = 0.05
TRACER_DIFF = 0.5

SUB = 8
LANES = 128
MESH = pl.DeviceIdType.MESH
SHARE = 2
EARLY = 2
AREA = 1.0 / (COARSEN * COARSEN)


def lane_index():
    return lax.broadcasted_iota(jnp.int32, (SUB, LANES), 1)


def following(v):
    lane = lane_index()
    wrapped = pltpu.roll(pltpu.roll(v, LANES - 1, 1), SUB - 1, 0)
    edge = jnp.where(lane < LANES - 1, pltpu.roll(v, LANES - SUB - 1, 1), wrapped)
    return jnp.where(lane < LANES - SUB, pltpu.roll(v, LANES - SUB, 1), edge)


def preceding(v):
    lane = lane_index()
    wrapped = pltpu.roll(pltpu.roll(v, 1, 1), 1, 0)
    edge = jnp.where(lane >= 1, pltpu.roll(v, SUB + 1, 1), wrapped)
    return jnp.where(lane >= SUB, pltpu.roll(v, SUB, 1), edge)


def to_right(v):
    return jnp.concatenate([v[1:], following(v[0])[None]], axis=0)


def to_left(v):
    return jnp.concatenate([preceding(v[COARSEN - 1])[None], v[:COARSEN - 1]], axis=0)


def exchange_lanes(rows):
    lane = lane_index()
    rows = list(rows)
    for step in (1, 2, 4):
        high = (lane & step) != 0
        for i in range(SUB):
            if not i & step:
                a, b = rows[i], rows[i | step]
                rows[i] = jnp.where(high, pltpu.roll(b, step, 1), a)
                rows[i | step] = jnp.where(high, b, pltpu.roll(a, LANES - step, 1))
    return rows


def exact_dot(x, w):
    rows = x.shape[0]
    hi = x.astype(jnp.bfloat16)
    rest = x - hi.astype(jnp.float32)
    mid = rest.astype(jnp.bfloat16)
    low = (rest - mid.astype(jnp.float32)).astype(jnp.bfloat16)
    y = jnp.dot(jnp.concatenate([hi.astype(jnp.float32), mid.astype(jnp.float32), low.astype(jnp.float32)], axis=0).astype(jnp.bfloat16), w,
                preferred_element_type=jnp.float32)
    return y[:rows] + y[rows:2 * rows] + y[2 * rows:]


def kernel(nt, nr, group, s_hbm, k_hbm, out_ref, nxt_ref,
           s_ref, k_ref, in_sem, wb, ub, own, kown, kh, kr, kl, kd, ku, ch, ct, part, order, ers, erg, cts, ctg, jall,
           vsend, vrecv, ksend, krecv, kfwd, ersend, errecv, ctsend, ctrecv, jsend, jrecv, tok_down, tok_up):
    t = lax.axis_index("tm")
    r = lax.axis_index("rows")
    member = lax.rem(t, group)
    base = t - member
    has_up = r > 0
    has_down = r < nr - 1
    sends = (has_down, has_up)
    gets = (has_up, has_down)
    f32 = jnp.float32

    k_in = pltpu.make_async_copy(k_hbm, k_ref, in_sem.at[0])
    s_in = pltpu.make_async_copy(s_hbm, s_ref, in_sem.at[1])
    k_in.start()
    s_in.start()

    barrier = pltpu.get_barrier_semaphore()

    def greet(tm, row):
        pl.semaphore_signal(barrier, inc=1, device_id=(tm, row), device_id_type=MESH)

    pl.when(has_up)(lambda: greet(t, r - 1))
    pl.when(has_down)(lambda: greet(t, r + 1))
    for o in range(1, nt):
        greet(lax.rem(t + o, nt), r)

    source = lax.broadcasted_iota(jnp.int32, order.shape, 0)
    target = lax.broadcasted_iota(jnp.int32, order.shape, 1)
    goes = (source & (SUB - 1)) * (LANES // SUB) + (source >> 3)
    order[...] = jnp.where(goes == target, 1.0, 0.0).astype(jnp.bfloat16)
    for d in range(1, FINE):
        zero = jnp.zeros(wb.shape[2:], f32)
        wb[(d - 1) % 2, SUB - d] = zero
        wb[(d - 1) % 2, 2 * SUB - 1 + d] = zero

    @pl.when(jnp.logical_not(has_up))
    def _():
        ub[0, 0:SUB] = jnp.zeros((SUB,) + ub.shape[2:], f32)
        kh[0] = jnp.zeros(kh.shape[1:], f32)

    @pl.when(jnp.logical_not(has_down))
    def _():
        ub[0, 2 * SUB:] = jnp.zeros((SUB,) + ub.shape[2:], f32)
        kh[1] = jnp.zeros(kh.shape[1:], f32)

    def read_row(ref, row):
        return jnp.stack(exchange_lanes(
            [ref[pl.ds(m * SUB + row, SUB, stride=SUB * SUB), :] for m in range(SUB)]), axis=0)

    outer_first = [row for d in range(SUB // 2) for row in (SUB - 1 - d, d)]

    k_in.wait()
    total = None
    for row in outer_first:
        x = read_row(k_ref, row)
        kown[row] = x
        total = x if total is None else total + x
    ers[0] = jnp.sum(total, axis=0) * AREA

    pl.semaphore_wait(barrier, (nt - 1) + has_up.astype(jnp.int32) + has_down.astype(jnp.int32))

    def tell(tok, row):
        pl.semaphore_signal(tok, inc=1, device_id=(t, row), device_id_type=MESH)

    pl.when(jnp.logical_not(has_up) & has_down)(lambda: tell(tok_down, r + 1))
    pl.when(jnp.logical_not(has_down) & has_up)(lambda: tell(tok_up, r - 1))

    def v_copy(side, d):
        if side == 0:
            return pltpu.make_async_remote_copy(
                own.at[SUB - d], ub.at[0, SUB - d], vsend.at[side, d - 1], vrecv.at[side, d - 1],
                device_id=(t, r + 1), device_id_type=MESH)
        return pltpu.make_async_remote_copy(
            own.at[d - 1], ub.at[0, 2 * SUB - 1 + d], vsend.at[side, d - 1], vrecv.at[side, d - 1],
            device_id=(t, r - 1), device_id_type=MESH)

    def k_copy(side, d):
        return pltpu.make_async_remote_copy(
            kown.at[SUB - d if side == 0 else d - 1], kh.at[side, d - 1], ksend.at[side, d - 1], krecv.at[side, d - 1],
            device_id=(t, r + 1 if side == 0 else r - 1), device_id_type=MESH)

    def k_forward(side, d, o):
        return pltpu.make_async_remote_copy(
            kh.at[side, d - 1], kh.at[side, d - 1], kfwd.at[side, d - 1, o], krecv.at[side, d - 1],
            device_id=(base + lax.rem(member + o, group), r), device_id_type=MESH)

    def mine(d):
        return member == (d - 1) % group

    def er_copy(o):
        return pltpu.make_async_remote_copy(
            ers, erg.at[r], ersend.at[o], errecv.at[o],
            device_id=(t, lax.rem(r + o, nr)), device_id_type=MESH)

    def ct_copy(o):
        return pltpu.make_async_remote_copy(
            cts, ctg.at[r], ctsend.at[o], ctrecv.at[o],
            device_id=(t, lax.rem(r + o, nr)), device_id_type=MESH)

    def j_copy(o):
        return pltpu.make_async_remote_copy(
            jall.at[t], jall.at[t], jsend.at[o], jrecv.at[t],
            device_id=(t + o, r), device_id_type=MESH)

    for d in range(1, FINE + 1):
        for side in range(2):
            pl.when(sends[side] & mine(d))(lambda: k_copy(side, d).start())

    s_in.wait()
    sums = [None, None]
    for row in outer_first:
        for f in range(2):
            x = read_row(s_ref.at[f], row)
            own[row, f] = x
            wb[0, SUB + row, f] = x
            ub[0, SUB + row, f] = x
            sums[f] = x if sums[f] is None else sums[f] + x
    for f in range(2):
        ers[1 + f] = jnp.sum(sums[f], axis=0) * AREA
    erg[r] = ers[...]

    def send_rows(first, last):
        for d in range(first, last + 1):
            for side in range(2):
                pl.when(sends[side])(lambda: v_copy(side, d).start())

    send_rows(1, EARLY)

    def columns_of(i, k):
        right = 0.5 * (k + to_right(k))
        kr[i] = right
        kl[i] = preceding(right[COARSEN - 1])

    def left_of(i):
        return jnp.concatenate([kl[i][None], kr[i, 0:COARSEN - 1]], axis=0)

    def centre_of(i):
        total = (kr[i] + left_of(i)) + (ku[i] + kd[i])
        ch[i] = (1.0 - EXCHANGE) - total
        ct[i] = (1.0 - EXCHANGE) - TRACER_DIFF * total

    for row in range(SUB):
        k = kown[row]
        columns_of(SUB + row, k)
        if row < SUB - 1:
            face = 0.5 * (k + kown[row + 1])
            kd[SUB + row] = face
            ku[SUB + row + 1] = face
        if 0 < row < SUB - 1:
            centre_of(SUB + row)

    def advance(buf, p, i, above=True, below=True):
        heat, tracer = buf[p, i, 0], buf[p, i, 1]
        right, left = kr[i], left_of(i)
        terms = [right * to_right(heat) + left * to_left(heat), right * to_right(tracer) + left * to_left(tracer)]
        if below:
            face = kd[i]
            terms = [terms[f] + face * buf[p, i + 1, f] for f in range(2)]
        if above:
            face = ku[i]
            terms = [terms[f] + face * buf[p, i - 1, f] for f in range(2)]
        return ((ch[i] * heat + EXCHANGE * tracer) + terms[0],
                (ct[i] * tracer + EXCHANGE * heat) + TRACER_DIFF * terms[1])

    for level in range(1, SUB // 2):
        p = (level - 1) % 2
        for row in range(level, SUB - level):
            heat, tracer = advance(wb, p, SUB + row)
            for f, x in enumerate((heat, tracer)):
                wb[1 - p, SUB + row, f] = x
                ub[1 - p, SUB + row, f] = x

    @pl.when(has_up)
    def _():
        pl.semaphore_wait(tok_down, 1)
        pl.when(has_down)(lambda: tell(tok_down, r + 1))

    @pl.when(has_down)
    def _():
        pl.semaphore_wait(tok_up, 1)
        pl.when(has_up)(lambda: tell(tok_up, r - 1))

    for o in range(1, nr):
        er_copy(o).start()

    def pass_on(d):
        for side in range(2):
            @pl.when(gets[side] & mine(d))
            def _():
                k_copy(side, d).wait_recv()
                for o in range(1, group):
                    k_forward(side, d, o).start()

    outside = (jnp.where(has_up, 1.0, 0.0), jnp.where(has_down, 1.0, 0.0))

    def faces_at(d):
        for side in range(2):
            pl.when(gets[side] & jnp.logical_not(mine(d)))(lambda: k_copy(side, d).wait_recv())
            k = kh[side, d - 1]
            inner = kh[side, d - 2] if d > 1 else kown[0 if side == 0 else SUB - 1]
            face = 0.5 * (k + inner)
            edge = face * outside[side] if d == 1 else face
            i = SUB - d if side == 0 else 2 * SUB - 1 + d
            columns_of(i, k)
            if side == 0:
                ku[i + 1] = face
                kd[i] = edge
                centre_of(i + 1)
            else:
                kd[i - 1] = face
                ku[i] = edge
                centre_of(i - 1)

    pass_on(1)
    for level in range(1, FINE):
        pass_on(level + 1)
        faces_at(level)
        p = (level - 1) % 2
        first, last = SUB + 1 - level, 2 * SUB - 2 + level
        for i in range(first, last + 1):
            if SUB + level <= i < 2 * SUB - level:
                continue
            heat, tracer = advance(wb, p, i)
            wb[1 - p, i, 0] = heat
            wb[1 - p, i, 1] = tracer
        for i, inner, face in ((first - 1, first, kd), (last + 1, last, ku)):
            for f in range(2):
                wb[1 - p, i, f] = (1.0, TRACER_DIFF)[f] * face[i] * wb[p, inner, f]

    p = (FINE - 1) % 2
    fluxes = [[jnp.sum(ku[SUB] * (wb[p, SUB - 1, f] - wb[p, SUB, f]), axis=0) for f in range(2)],
              [jnp.sum(kd[2 * SUB - 1] * (wb[p, 2 * SUB, f] - wb[p, 2 * SUB - 1, f]), axis=0) for f in range(2)]]
    for b in range(3):
        whole, gain = [], []
        for f in range(2):
            total, side_flux = None, None
            for i in range(max(1, SUB * b), min(3 * SUB - 1, SUB * (b + 1))):
                x = wb[p, i, f]
                flux = kr[i, COARSEN - 1] * (following(x[0]) - x[COARSEN - 1])
                total = x if total is None else total + x
                side_flux = flux if side_flux is None else side_flux + flux
            change = side_flux - preceding(side_flux)
            if b == 0:
                change = change - fluxes[0][f]
            elif b == 1:
                change = change + (fluxes[0][f] + fluxes[1][f])
            else:
                change = change - fluxes[1][f]
            whole.append(jnp.sum(total, axis=0))
            gain.append((1.0, TRACER_DIFF)[f] * change)
        moved = EXCHANGE * (whole[1] - whole[0])
        cts[b, 0] = AREA * ((whole[0] + moved) + gain[0])
        cts[b, 1] = AREA * ((whole[1] - moved) + gain[1])
    for o in range(1, nr):
        ct_copy(o).start()
    ctg[r] = cts[...]
    send_rows(EARLY + 1, FINE)

    faces_at(FINE)

    def row_pair(level, diagonal):
        p = lax.rem(level + 1, 2)
        new = [(i,) + advance(ub, p, i) for i in (SUB + level - diagonal, 2 * SUB - 1 - level + diagonal)]
        for i, heat, tracer in new:
            ub[1 - p, i, 0] = heat
            ub[1 - p, i, 1] = tracer

    def run_diagonal(diagonal):
        for side in range(2):
            pl.when(gets[side])(lambda: v_copy(side, diagonal).wait_recv())

        def step(level, carry):
            row_pair(level, diagonal)
            return carry
        lax.fori_loop(1, min(FINE, SUB // 2 - 1 + diagonal) + 1, step, 0)

    ratio = (FINE / COARSE) / float(COARSEN * COARSEN)
    rate = EXCHANGE * (FINE / COARSE)

    run_diagonal(1)
    run_diagonal(2)

    for o in range(1, nr):
        er_copy(o).wait_recv()
    kcv = [erg[i, 0] for i in range(nr)]
    c_right = [ratio * 0.5 * (k + following(k)) for k in kcv]
    c_left = [ratio * 0.5 * (k + preceding(k)) for k in kcv]
    c_face = [ratio * 0.5 * kcv[0]]
    c_face += [ratio * 0.5 * (kcv[i] + kcv[i + 1]) for i in range(nr - 1)]
    c_face += [ratio * 0.5 * kcv[nr - 1]]
    totals = [(c_right[i] + c_left[i]) + (c_face[i] + c_face[i + 1]) for i in range(nr)]
    c_centre = [[(1.0 - rate) - x for x in totals], [(1.0 - rate) - TRACER_DIFF * x for x in totals]]

    def coarse_prop(state):
        for substep in range(COARSE):
            new = []
            for f in range(2):
                rows = state[f * nr:(f + 1) * nr]
                other = state[(1 - f) * nr:(2 - f) * nr]
                for i in range(nr):
                    v = rows[i]
                    around = c_right[i] * following(v) + c_left[i] * preceding(v)
                    if i > 0:
                        around = around + c_face[i] * rows[i - 1]
                    if i < nr - 1:
                        around = around + c_face[i + 1] * rows[i + 1]
                    if f == 1:
                        around = TRACER_DIFF * around
                    new.append((c_centre[f][i] * v + rate * other[i]) + around)
            state = tuple(new)
        return state

    later = jnp.where(t > 0, 1.0, 0.0)
    old = coarse_prop(tuple(later * erg[i, 1 + f] for f in range(2) for i in range(nr)))

    for o in range(1, nr):
        ct_copy(o).wait_recv()
    change = []
    for f in range(2):
        for i in range(nr):
            x = ctg[i, 1, f]
            if i > 0:
                x = x + ctg[i - 1, 2, f]
            if i < nr - 1:
                x = x + ctg[i + 1, 0, f]
            x = x - old[f * nr + i]
            jall[t, i, f] = x
            change.append(x)
    for o in range(1, nt):
        pl.when(t + o < nt)(lambda: j_copy(o).start())

    for d in range(3, FINE):
        run_diagonal(d)

    def place(level, side):
        return level if side == 0 else 3 * SUB - 1 - level

    for level in range(1, FINE + 1):
        for side in range(2):
            heat, tracer = advance(ub, (level - 1) % 2, place(level, side), above=side == 1, below=side == 0)
            part[level - 1, side, 0] = heat
            part[level - 1, side, 1] = tracer

    def link(n, state):
        pltpu.make_async_remote_copy(
            jall.at[n], jall.at[n], jsend.at[0], jrecv.at[n],
            device_id=(n, r), device_id_type=MESH).wait_recv()
        state = coarse_prop(state)
        return tuple(state[f * nr + i] + jall[n, i, f] for f in range(2) for i in range(nr))

    state = tuple(jnp.zeros((SUB, LANES), f32) for _ in range(2 * nr))
    state = lax.fori_loop(0, t, link, state)
    state = coarse_prop(state)

    fix = [None, None]
    for f in range(2):
        for i in range(nr):
            value = state[f * nr + i] - old[f * nr + i]
            fix[f] = value if i == 0 else jnp.where(r == i, value, fix[f])
    natural = exact_dot(jnp.concatenate([state[n] + change[n] for n in range(2 * nr)], axis=0), order[...])
    for f in range(2):
        for i in range(nr):
            n = f * nr + i
            nxt_ref[f, pl.ds(i, SUB, stride=nr), :] = natural[n * SUB:(n + 1) * SUB]

    def write_row(row, f, end):
        end = exchange_lanes([end[m] + fix[f] for m in range(COARSEN)])
        for m in range(SUB):
            out_ref[f, pl.ds(m * SUB + row, SUB, stride=SUB * SUB), :] = end[m]

    for row in range(1, SUB - 1):
        for f in range(2):
            write_row(row, f, ub[0, SUB + row, f])

    last = []
    for side in range(2):
        pl.when(gets[side])(lambda: v_copy(side, FINE).wait_recv())
    for side in range(2):
        i = place(0, side)
        last.append([ub[0, i, 0], ub[0, i, 1]])
    for level in range(1, FINE + 1):
        for side in range(2):
            face = (ku, kd)[side][place(level, side)]
            heat, tracer = last[side]
            last[side] = [part[level - 1, side, 0] + face * heat,
                          part[level - 1, side, 1] + (TRACER_DIFF * face) * tracer]
    for side in range(2):
        for f in range(2):
            write_row((0, SUB - 1)[side], f, last[side][f])

    for d in range(1, FINE + 1):
        for side in range(2):
            pl.when(sends[side])(lambda: v_copy(side, d).wait_send())
            pl.when(sends[side] & mine(d))(lambda: k_copy(side, d).wait_send())

            @pl.when(gets[side] & mine(d))
            def _():
                for o in range(1, group):
                    k_forward(side, d, o).wait_send()
    for o in range(1, nr):
        er_copy(o).wait_send()
        ct_copy(o).wait_send()
    for o in range(1, nt):
        pl.when(t + o < nt)(lambda: j_copy(o).wait_send())


def deliver(ends, following, ends_out, following_out, sem):
    first = pltpu.make_async_copy(ends, ends_out, sem.at[0])
    second = pltpu.make_async_copy(following, following_out, sem.at[1])
    first.start()
    second.start()
    first.wait()
    second.wait()


def body(nt, nr, starts, conductivity):
    rows, columns = conductivity.shape
    assert rows == SUB == COARSEN == FINE
    assert columns == COARSEN * SUB * LANES
    blocks = columns // LANES
    group = math.gcd(SHARE, nt)
    slab = starts[0].reshape(2, rows, blocks, LANES).transpose(0, 2, 1, 3).reshape(2, blocks * rows, LANES)
    kappa = conductivity.reshape(rows, blocks, LANES).transpose(1, 0, 2).reshape(blocks * rows, LANES)
    slab = pltpu.with_memory_space_constraint(slab, pltpu.HBM)
    kappa = pltpu.with_memory_space_constraint(kappa, pltpu.HBM)
    f32 = jnp.float32
    dma = pltpu.SemaphoreType.DMA
    cell = (SUB, LANES)
    line = (COARSEN,) + cell
    ends, following = pl.pallas_call(
        functools.partial(kernel, nt, nr, group),
        out_shape=(
            jax.ShapeDtypeStruct((2, blocks * rows, LANES), f32),
            jax.ShapeDtypeStruct((2, SUB * nr, LANES), f32),
        ),
        in_specs=[pl.BlockSpec(memory_space=pltpu.HBM)] * 2,
        out_specs=[pl.BlockSpec(memory_space=pltpu.VMEM)] * 2,
        scratch_shapes=[
            pltpu.VMEM((2, blocks * rows, LANES), f32),
            pltpu.VMEM((blocks * rows, LANES), f32),
            dma((2,)),
            pltpu.VMEM((2, 3 * SUB, 2) + line, f32),
            pltpu.VMEM((2, 3 * SUB, 2) + line, f32),
            pltpu.VMEM((SUB, 2) + line, f32),
            pltpu.VMEM((SUB,) + line, f32),
            pltpu.VMEM((2, FINE) + line, f32),
            pltpu.VMEM((3 * SUB,) + line, f32),
            pltpu.VMEM((3 * SUB,) + cell, f32),
            pltpu.VMEM((3 * SUB,) + line, f32),
            pltpu.VMEM((3 * SUB,) + line, f32),
            pltpu.VMEM((3 * SUB,) + line, f32),
            pltpu.VMEM((3 * SUB,) + line, f32),
            pltpu.VMEM((FINE, 2, 2) + line, f32),
            pltpu.VMEM((LANES, LANES), jnp.bfloat16),
            pltpu.VMEM((3,) + cell, f32),
            pltpu.VMEM((nr, 3) + cell, f32),
            pltpu.VMEM((3, 2) + cell, f32),
            pltpu.VMEM((nr, 3, 2) + cell, f32),
            pltpu.VMEM((nt, nr, 2) + cell, f32),
            dma((2, FINE)), dma((2, FINE)),
            dma((2, FINE)), dma((2, FINE)), dma((2, FINE, group)),
            dma((nr,)), dma((nr,)),
            dma((nr,)), dma((nr,)),
            dma((nt,)), dma((nt,)),
            pltpu.SemaphoreType.REGULAR, pltpu.SemaphoreType.REGULAR,
        ],
        compiler_params=pltpu.CompilerParams(
            collective_id=0, has_side_effects=True, vmem_limit_bytes=48 * 1024 * 1024),
        name="parareal",
    )(slab, kappa)
    ends, following = pl.pallas_call(
        deliver,
        out_shape=(
            jax.ShapeDtypeStruct(ends.shape, f32),
            jax.ShapeDtypeStruct(following.shape, f32),
        ),
        in_specs=[pl.BlockSpec(memory_space=pltpu.VMEM)] * 2,
        out_specs=[pl.BlockSpec(memory_space=pltpu.HBM)] * 2,
        scratch_shapes=[dma((2,))],
        compiler_params=pltpu.CompilerParams(vmem_limit_bytes=1024 * 1024),
        name="deliver",
    )(ends, following)
    new_ends = ends.reshape(2, blocks, rows, LANES).transpose(0, 2, 1, 3).reshape(2, rows, columns)
    coarse_next = following.reshape(2, SUB, nr, LANES).transpose(0, 2, 1, 3).reshape(2, nr, SUB * LANES)
    return new_ends[None], coarse_next[None]


def solution(mesh):
    nt, nr = mesh.shape["tm"], mesh.shape["rows"]
    in_specs = (P("tm", None, "rows", None), P("rows", None))
    out_specs = (P("tm", None, "rows", None), P("tm", None, None, None))
    return jax.shard_map(functools.partial(body, nt, nr), mesh=mesh, in_specs=in_specs, out_specs=out_specs, check_vma=False)
```

time: 32.5 us -> 30.4 us (0.935)
  the two profiles are of different devices: /device:TPU:5 before, /device:TPU:0 now
where the time goes in v2:
time: 30.4 us; the launch traced here: 30.2 us
  Pallas kernels  29.6 us (97%)
  between operations  0.64 us (2%)
    pallas_call x1, Pallas kernels, body(): pl.pallas_call(functools.partial(kernel, nt, nr, group), out_shape=(jax.S...  28.8 us
    pallas_call x1, Pallas kernels, body(): pl.pallas_call(deliver, out_shape=(jax.ShapeDtypeStruct(ends.shape, f32),...  0.81 us

profile of v2, /device:TPU:0, one launch (start us, length us, event | category | flops | bytes accessed | tf_op | source)
XLA Modules:
  0.0 30.2 jit_solution(11463300351991550419)
XLA Ops:
  0.6 28.8 %parareal.1 = (f32[2,512,128]{2,1,0:T(8,128)S(1)}, f32[2,32,128]{2,1,0:T(8,128)S(1)}) custom-call(f32[2,512,128]{2,1,0:T(8,128)} %bitcast.20, f32[512,128]{1,0:T(8,128)} %bitcast.21), custom_call_target="tpu_custom_call" | custom-call | tf_op jit(solution)/shard_map/parareal/pallas_call | solution.py:506
  29.4 0.8 %deliver.1 = (f32[2,512,128]{2,1,0:T(8,128)}, f32[2,32,128]{2,1,0:T(8,128)}) custom-call(f32[2,512,128]{2,1,0:T(8,128)S(1)} %get-tuple-element.6.ends, f32[2,32,128]{2,1,0:T(8,128)S(1)} %get-tuple-element.7.following), custom_call_target="tpu_custom_call" | custom-call | tf_op jit(solution)/shard_map/deliver/pallas_call | solution.py:547

commit v3 on v2

--- a/solution.py
+++ b/solution.py
@@ -18,26 +18,39 @@
 LANES = 128
 MESH = pl.DeviceIdType.MESH
 SHARE = 2
-EARLY = 2
+EARLY = 3
+SLOTS = 3
 AREA = 1.0 / (COARSEN * COARSEN)
 
 
-def lane_index():
-    return lax.broadcasted_iota(jnp.int32, (SUB, LANES), 1)
+def cell_index(axis):
+    return lax.broadcasted_iota(jnp.int32, (SUB, LANES), axis)
 
 
 def following(v):
-    lane = lane_index()
-    wrapped = pltpu.roll(pltpu.roll(v, LANES - 1, 1), SUB - 1, 0)
-    edge = jnp.where(lane < LANES - 1, pltpu.roll(v, LANES - SUB - 1, 1), wrapped)
-    return jnp.where(lane < LANES - SUB, pltpu.roll(v, LANES - SUB, 1), edge)
+    lane = cell_index(1)
+    near = pltpu.roll(v, LANES - SUB, 1)
+    far = jnp.where(lane < LANES - 1, pltpu.roll(v, LANES - SUB - 1, 1), pltpu.roll(v, LANES - 1, 1))
+    edge = pltpu.roll(jnp.where(cell_index(0) == 0, far, near), SUB - 1, 0)
+    return jnp.where(lane < LANES - SUB, near, edge)
 
 
 def preceding(v):
-    lane = lane_index()
-    wrapped = pltpu.roll(pltpu.roll(v, 1, 1), 1, 0)
-    edge = jnp.where(lane >= 1, pltpu.roll(v, SUB + 1, 1), wrapped)
-    return jnp.where(lane >= SUB, pltpu.roll(v, SUB, 1), edge)
+    lane = cell_index(1)
+    near = pltpu.roll(v, SUB, 1)
+    far = jnp.where(lane >= 1, pltpu.roll(v, SUB + 1, 1), pltpu.roll(v, 1, 1))
+    edge = pltpu.roll(jnp.where(cell_index(0) == SUB - 1, far, near), 1, 0)
+    return jnp.where(lane >= SUB, near, edge)
+
+
+def lines_to_lanes(v):
+    lane, line = cell_index(1), cell_index(0)
+    for step in (1, 2, 4):
+        high_lane, high_line = (lane & (step * 16)) != 0, (line & step) != 0
+        up = pltpu.roll(pltpu.roll(v, SUB - step, 0), step * 16, 1)
+        down = pltpu.roll(pltpu.roll(v, step, 0), LANES - step * 16, 1)
+        v = jnp.where(high_lane, jnp.where(high_line, v, up), jnp.where(high_line, down, v))
+    return v
 
 
 def to_right(v):
@@ -49,7 +62,7 @@
 
 
 def exchange_lanes(rows):
-    lane = lane_index()
+    lane = cell_index(1)
     rows = list(rows)
     for step in (1, 2, 4):
         high = (lane & step) != 0
@@ -74,7 +87,7 @@
 
 def kernel(nt, nr, group, s_hbm, k_hbm, out_ref, nxt_ref,
            s_ref, k_ref, in_sem, wb, ub, own, kown, kh, kr, kl, kd, ku, ch, ct, part, order, ers, erg, cts, ctg, jall,
-           vsend, vrecv, ksend, krecv, kfwd, ersend, errecv, ctsend, ctrecv, jsend, jrecv, tok_down, tok_up):
+           vsend, vrecv, ksend, krecv, kfwd, ersend, errecv, ctsend, ctrecv, jsend, jrecv, tok_down, tok_up, tok_tm):
     t = lax.axis_index("tm")
     r = lax.axis_index("rows")
     member = lax.rem(t, group)
@@ -85,6 +98,8 @@
     gets = (has_up, has_down)
     f32 = jnp.float32
 
+    outer_first = [row for d in range(SUB // 2) for row in (SUB - 1 - d, d)]
+
     k_in = pltpu.make_async_copy(k_hbm, k_ref, in_sem.at[0])
     s_in = pltpu.make_async_copy(s_hbm, s_ref, in_sem.at[1])
     k_in.start()
@@ -98,7 +113,9 @@
     pl.when(has_up)(lambda: greet(t, r - 1))
     pl.when(has_down)(lambda: greet(t, r + 1))
     for o in range(1, nt):
-        greet(lax.rem(t + o, nt), r)
+        pl.when(t + o < nt)(lambda: greet(t + o, r))
+    for o in range(1, group):
+        pl.when(member >= o)(lambda: greet(t - o, r))
 
     source = lax.broadcasted_iota(jnp.int32, order.shape, 0)
     target = lax.broadcasted_iota(jnp.int32, order.shape, 1)
@@ -121,9 +138,7 @@
 
     def read_row(ref, row):
         return jnp.stack(exchange_lanes(
-            [ref[pl.ds(m * SUB + row, SUB, stride=SUB * SUB), :] for m in range(SUB)]), axis=0)
-
-    outer_first = [row for d in range(SUB // 2) for row in (SUB - 1 - d, d)]
+            [ref[pl.ds(m * SUB * SUB + row, SUB, stride=SUB), :] for m in range(SUB)]), axis=0)
 
     k_in.wait()
     total = None
@@ -133,13 +148,29 @@
         total = x if total is None else total + x
     ers[0] = jnp.sum(total, axis=0) * AREA
 
-    pl.semaphore_wait(barrier, (nt - 1) + has_up.astype(jnp.int32) + has_down.astype(jnp.int32))
+    pl.semaphore_wait(barrier, t + (group - 1 - member) + has_up.astype(jnp.int32) + has_down.astype(jnp.int32))
 
     def tell(tok, row):
         pl.semaphore_signal(tok, inc=1, device_id=(t, row), device_id_type=MESH)
 
     pl.when(jnp.logical_not(has_up) & has_down)(lambda: tell(tok_down, r + 1))
     pl.when(jnp.logical_not(has_down) & has_up)(lambda: tell(tok_up, r - 1))
+
+    for o in range(1, nt):
+        @pl.when(t >= o)
+        def _():
+            pl.semaphore_signal(tok_tm, inc=1, device_id=(t - o, r), device_id_type=MESH)
+
+    def relay(slot):
+        @pl.when(has_up & (jnp.minimum(r - 1, SLOTS - 1) == slot))
+        def _():
+            pl.semaphore_wait(tok_down, 1)
+            pl.when(has_down)(lambda: tell(tok_down, r + 1))
+
+        @pl.when(has_down & (jnp.minimum(nr - 2 - r, SLOTS - 1) == slot))
+        def _():
+            pl.semaphore_wait(tok_up, 1)
+            pl.when(has_up)(lambda: tell(tok_up, r - 1))
 
     def v_copy(side, d):
         if side == 0:
@@ -238,6 +269,7 @@
         return ((ch[i] * heat + EXCHANGE * tracer) + terms[0],
                 (ct[i] * tracer + EXCHANGE * heat) + TRACER_DIFF * terms[1])
 
+    relay(0)
     for level in range(1, SUB // 2):
         p = (level - 1) % 2
         for row in range(level, SUB - level):
@@ -245,19 +277,6 @@
             for f, x in enumerate((heat, tracer)):
                 wb[1 - p, SUB + row, f] = x
                 ub[1 - p, SUB + row, f] = x
-
-    @pl.when(has_up)
-    def _():
-        pl.semaphore_wait(tok_down, 1)
-        pl.when(has_down)(lambda: tell(tok_down, r + 1))
-
-    @pl.when(has_down)
-    def _():
-        pl.semaphore_wait(tok_up, 1)
-        pl.when(has_up)(lambda: tell(tok_up, r - 1))
-
-    for o in range(1, nr):
-        er_copy(o).start()
 
     def pass_on(d):
         for side in range(2):
@@ -291,6 +310,11 @@
     for level in range(1, FINE):
         pass_on(level + 1)
         faces_at(level)
+        if level in (2, 4):
+            relay(level // 2)
+        if level == 4:
+            for o in range(1, nr):
+                er_copy(o).start()
         p = (level - 1) % 2
         first, last = SUB + 1 - level, 2 * SUB - 2 + level
         for i in range(first, last + 1):
@@ -402,6 +426,7 @@
             x = x - old[f * nr + i]
             jall[t, i, f] = x
             change.append(x)
+    pl.when(t < nt - 1)(lambda: pl.semaphore_wait(tok_tm, nt - 1 - t))
     for o in range(1, nt):
         pl.when(t + o < nt)(lambda: j_copy(o).start())
 
@@ -437,12 +462,12 @@
     for f in range(2):
         for i in range(nr):
             n = f * nr + i
-            nxt_ref[f, pl.ds(i, SUB, stride=nr), :] = natural[n * SUB:(n + 1) * SUB]
+            nxt_ref[f, pl.ds(i, SUB, stride=nr), :] = lines_to_lanes(natural[n * SUB:(n + 1) * SUB])
 
     def write_row(row, f, end):
         end = exchange_lanes([end[m] + fix[f] for m in range(COARSEN)])
         for m in range(SUB):
-            out_ref[f, pl.ds(m * SUB + row, SUB, stride=SUB * SUB), :] = end[m]
+            out_ref[f, row, m * SUB:(m + 1) * SUB, :] = end[m]
 
     for row in range(1, SUB - 1):
         for f in range(2):
@@ -481,12 +506,14 @@
 
 
 def deliver(ends, following, ends_out, following_out, sem):
-    first = pltpu.make_async_copy(ends, ends_out, sem.at[0])
-    second = pltpu.make_async_copy(following, following_out, sem.at[1])
-    first.start()
-    second.start()
-    first.wait()
-    second.wait()
+    fields, rows = ends.shape[:2]
+    copies = [pltpu.make_async_copy(ends.at[f, row], ends_out.at[f, :, row, :], sem.at[f * rows + row])
+              for row in range(rows) for f in range(fields)]
+    copies.append(pltpu.make_async_copy(following, following_out, sem.at[fields * rows]))
+    for copy in copies:
+        copy.start()
+    for copy in copies:
+        copy.wait()
 
 
 def body(nt, nr, starts, conductivity):
@@ -506,7 +533,7 @@
     ends, following = pl.pallas_call(
         functools.partial(kernel, nt, nr, group),
         out_shape=(
-            jax.ShapeDtypeStruct((2, blocks * rows, LANES), f32),
+            jax.ShapeDtypeStruct((2, rows, blocks, LANES), f32),
             jax.ShapeDtypeStruct((2, SUB * nr, LANES), f32),
         ),
         in_specs=[pl.BlockSpec(memory_space=pltpu.HBM)] * 2,
@@ -538,7 +565,7 @@
             dma((nr,)), dma((nr,)),
             dma((nr,)), dma((nr,)),
             dma((nt,)), dma((nt,)),
-            pltpu.SemaphoreType.REGULAR, pltpu.SemaphoreType.REGULAR,
+            pltpu.SemaphoreType.REGULAR, pltpu.SemaphoreType.REGULAR, pltpu.SemaphoreType.REGULAR,
         ],
         compiler_params=pltpu.CompilerParams(
             collective_id=0, has_side_effects=True, vmem_limit_bytes=48 * 1024 * 1024),
@@ -547,16 +574,16 @@
     ends, following = pl.pallas_call(
         deliver,
         out_shape=(
-            jax.ShapeDtypeStruct(ends.shape, f32),
+            jax.ShapeDtypeStruct((2, blocks, rows, LANES), f32),
             jax.ShapeDtypeStruct(following.shape, f32),
         ),
         in_specs=[pl.BlockSpec(memory_space=pltpu.VMEM)] * 2,
         out_specs=[pl.BlockSpec(memory_space=pltpu.HBM)] * 2,
-        scratch_shapes=[dma((2,))],
+        scratch_shapes=[dma((2 * rows + 1,))],
         compiler_params=pltpu.CompilerParams(vmem_limit_bytes=1024 * 1024),
         name="deliver",
     )(ends, following)
-    new_ends = ends.reshape(2, blocks, rows, LANES).transpose(0, 2, 1, 3).reshape(2, rows, columns)
+    new_ends = ends.transpose(0, 2, 1, 3).reshape(2, rows, columns)
     coarse_next = following.reshape(2, SUB, nr, LANES).transpose(0, 2, 1, 3).reshape(2, nr, SUB * LANES)
     return new_ends[None], coarse_next[None]
 

time: 30.4 us -> 28.3 us (0.931)
  Pallas kernels: 29.6 us -> 27.2 us
    pallas_call x1, Pallas kernels: 28.8 us -> 26.3 us  [body(): pl.pallas_call(functools.partial(kernel, nt, nr, group), out_shape=(jax.S...]
where the time goes in v3:
time: 28.3 us; the launch traced here: 27.8 us
  Pallas kernels  27.2 us (96%)
  between operations  0.64 us (2%)
    pallas_call x1, Pallas kernels, body(): pl.pallas_call(functools.partial(kernel, nt, nr, group), out_shape=(jax.S...  26.3 us
    pallas_call x1, Pallas kernels, body(): pl.pallas_call(deliver, out_shape=(jax.ShapeDtypeStruct((2, blocks, rows,...  0.94 us

profile of v3, /device:TPU:0, one launch (start us, length us, event | category | flops | bytes accessed | tf_op | source)
XLA Modules:
  0.0 27.8 jit_solution(13016188274305559456)
XLA Ops:
  0.6 26.3 %parareal.1 = (f32[2,8,64,128]{3,2,1,0:T(8,128)S(1)}, f32[2,32,128]{2,1,0:T(8,128)S(1)}) custom-call(f32[2,512,128]{2,1,0:T(8,128)} %bitcast.18, f32[512,128]{1,0:T(8,128)} %bitcast.19), custom_call_target="tpu_custom_call" | custom-call | tf_op jit(solution)/shard_map/parareal/pallas_call | solution.py:533
  26.9 0.9 %deliver.1 = (f32[2,64,8,128]{3,2,1,0:T(8,128)}, f32[2,32,128]{2,1,0:T(8,128)}) custom-call(f32[2,8,64,128]{3,2,1,0:T(8,128)S(1)} %get-tuple-element.6.ends, f32[2,32,128]{2,1,0:T(8,128)S(1)} %get-tuple-element.7.following), custom_call_target="tpu_custom_call" | custom-call | tf_op jit(solution)/shard_map/deliver/pallas_call | solution.py:574

commit v4 on v3

--- a/solution.py
+++ b/solution.py
@@ -18,7 +18,7 @@
 LANES = 128
 MESH = pl.DeviceIdType.MESH
 SHARE = 2
-EARLY = 3
+EARLY = 4
 SLOTS = 3
 AREA = 1.0 / (COARSEN * COARSEN)
 
@@ -175,20 +175,20 @@
     def v_copy(side, d):
         if side == 0:
             return pltpu.make_async_remote_copy(
-                own.at[SUB - d], ub.at[0, SUB - d], vsend.at[side, d - 1], vrecv.at[side, d - 1],
+                own.at[SUB - d], ub.at[0, SUB - d], vsend.at[side], vrecv.at[side, d - 1],
                 device_id=(t, r + 1), device_id_type=MESH)
         return pltpu.make_async_remote_copy(
-            own.at[d - 1], ub.at[0, 2 * SUB - 1 + d], vsend.at[side, d - 1], vrecv.at[side, d - 1],
+            own.at[d - 1], ub.at[0, 2 * SUB - 1 + d], vsend.at[side], vrecv.at[side, d - 1],
             device_id=(t, r - 1), device_id_type=MESH)
 
     def k_copy(side, d):
         return pltpu.make_async_remote_copy(
-            kown.at[SUB - d if side == 0 else d - 1], kh.at[side, d - 1], ksend.at[side, d - 1], krecv.at[side, d - 1],
+            kown.at[SUB - d if side == 0 else d - 1], kh.at[side, d - 1], ksend.at[side], krecv.at[side, d - 1],
             device_id=(t, r + 1 if side == 0 else r - 1), device_id_type=MESH)
 
     def k_forward(side, d, o):
         return pltpu.make_async_remote_copy(
-            kh.at[side, d - 1], kh.at[side, d - 1], kfwd.at[side, d - 1, o], krecv.at[side, d - 1],
+            kh.at[side, d - 1], kh.at[side, d - 1], kfwd.at[side], krecv.at[side, d - 1],
             device_id=(base + lax.rem(member + o, group), r), device_id_type=MESH)
 
     def mine(d):
@@ -196,12 +196,12 @@
 
     def er_copy(o):
         return pltpu.make_async_remote_copy(
-            ers, erg.at[r], ersend.at[o], errecv.at[o],
+            ers, erg.at[r], ersend, errecv.at[o],
             device_id=(t, lax.rem(r + o, nr)), device_id_type=MESH)
 
     def ct_copy(o):
         return pltpu.make_async_remote_copy(
-            cts, ctg.at[r], ctsend.at[o], ctrecv.at[o],
+            cts, ctg.at[r], ctsend, ctrecv.at[o],
             device_id=(t, lax.rem(r + o, nr)), device_id_type=MESH)
 
     def j_copy(o):
@@ -230,8 +230,6 @@
         for d in range(first, last + 1):
             for side in range(2):
                 pl.when(sends[side])(lambda: v_copy(side, d).start())
-
-    send_rows(1, EARLY)
 
     def columns_of(i, k):
         right = 0.5 * (k + to_right(k))
@@ -310,6 +308,8 @@
     for level in range(1, FINE):
         pass_on(level + 1)
         faces_at(level)
+        if level == 1:
+            send_rows(1, EARLY)
         if level in (2, 4):
             relay(level // 2)
         if level == 4:
@@ -354,8 +354,6 @@
     for o in range(1, nr):
         ct_copy(o).start()
     ctg[r] = cts[...]
-    send_rows(EARLY + 1, FINE)
-
     faces_at(FINE)
 
     def row_pair(level, diagonal):
@@ -368,6 +366,8 @@
     def run_diagonal(diagonal):
         for side in range(2):
             pl.when(gets[side])(lambda: v_copy(side, diagonal).wait_recv())
+        if diagonal != 3:
+            send_rows(diagonal + EARLY, min(diagonal + EARLY, FINE))
 
         def step(level, carry):
             row_pair(level, diagonal)
@@ -379,6 +379,7 @@
 
     run_diagonal(1)
     run_diagonal(2)
+    send_rows(EARLY + 3, EARLY + 3)
 
     for o in range(1, nr):
         er_copy(o).wait_recv()
@@ -442,6 +443,30 @@
             part[level - 1, side, 0] = heat
             part[level - 1, side, 1] = tracer
 
+    share = FINE // group
+    for side in range(2):
+        @pl.when(sends[side])
+        def _():
+            pltpu.make_async_remote_copy(
+                kown.at[pl.ds(0, share)], kh.at[side, pl.ds(0, share)], ksend.at[side], krecv.at[side, 0],
+                device_id=(t, r + 1 if side == 0 else r - 1), device_id_type=MESH).wait_send()
+
+        if group > 1:
+            @pl.when(gets[side])
+            def _():
+                passed = kh.at[side, pl.ds(0, share * (group - 1))]
+                pltpu.make_async_remote_copy(
+                    passed, passed, kfwd.at[side], krecv.at[side, 0],
+                    device_id=(base + lax.rem(member + 1, group), r), device_id_type=MESH).wait_send()
+    if nr > 1:
+        for ref, send, recv in ((erg, ersend, errecv), (ctg, ctsend, ctrecv)):
+            spread = ref.at[pl.ds(0, nr - 1)]
+            pltpu.make_async_remote_copy(
+                spread, spread, send, recv.at[0],
+                device_id=(t, lax.rem(r + 1, nr)), device_id_type=MESH).wait_send()
+    for o in range(1, nt):
+        pl.when(t + o < nt)(lambda: j_copy(o).wait_send())
+
     def link(n, state):
         pltpu.make_async_remote_copy(
             jall.at[n], jall.at[n], jsend.at[0], jrecv.at[n],
@@ -489,20 +514,12 @@
         for f in range(2):
             write_row((0, SUB - 1)[side], f, last[side][f])
 
-    for d in range(1, FINE + 1):
-        for side in range(2):
-            pl.when(sends[side])(lambda: v_copy(side, d).wait_send())
-            pl.when(sends[side] & mine(d))(lambda: k_copy(side, d).wait_send())
-
-            @pl.when(gets[side] & mine(d))
-            def _():
-                for o in range(1, group):
-                    k_forward(side, d, o).wait_send()
-    for o in range(1, nr):
-        er_copy(o).wait_send()
-        ct_copy(o).wait_send()
-    for o in range(1, nt):
-        pl.when(t + o < nt)(lambda: j_copy(o).wait_send())
+    for side in range(2):
+        @pl.when(sends[side])
+        def _():
+            pltpu.make_async_remote_copy(
+                own, ub.at[0, pl.ds(0, SUB)], vsend.at[side], vrecv.at[side, 0],
+                device_id=(t, r + 1 if side == 0 else r - 1), device_id_type=MESH).wait_send()
 
 
 def deliver(ends, following, ends_out, following_out, sem):
@@ -560,10 +577,10 @@
             pltpu.VMEM((3, 2) + cell, f32),
             pltpu.VMEM((nr, 3, 2) + cell, f32),
             pltpu.VMEM((nt, nr, 2) + cell, f32),
-            dma((2, FINE)), dma((2, FINE)),
-            dma((2, FINE)), dma((2, FINE)), dma((2, FINE, group)),
-            dma((nr,)), dma((nr,)),
-            dma((nr,)), dma((nr,)),
+            dma((2,)), dma((2, FINE)),
+            dma((2,)), dma((2, FINE)), dma((2,)),
+            dma, dma((nr,)),
+            dma, dma((nr,)),
             dma((nt,)), dma((nt,)),
             pltpu.SemaphoreType.REGULAR, pltpu.SemaphoreType.REGULAR, pltpu.SemaphoreType.REGULAR,
         ],

time: 28.3 us -> 28.6 us (1.011)
  the two profiles are of different devices: /device:TPU:0 before, /device:TPU:15 now
where the time goes in v4:
time: 28.6 us; the launch traced here: 28.4 us
  Pallas kernels  27.8 us (97%)
  between operations  0.64 us (2%)
    pallas_call x1, Pallas kernels, body(): pl.pallas_call(functools.partial(kernel, nt, nr, group), out_shape=(jax.S...  26.8 us
    pallas_call x1, Pallas kernels, body(): pl.pallas_call(deliver, out_shape=(jax.ShapeDtypeStruct((2, blocks, rows,...  0.94 us

profile of v4, /device:TPU:15, one launch (start us, length us, event | category | flops | bytes accessed | tf_op | source)
XLA Modules:
  0.0 28.4 jit_solution(9847267410810454327)
XLA Ops:
  0.6 26.8 %parareal.1 = (f32[2,8,64,128]{3,2,1,0:T(8,128)S(1)}, f32[2,32,128]{2,1,0:T(8,128)S(1)}) custom-call(f32[2,512,128]{2,1,0:T(8,128)} %bitcast.18, f32[512,128]{1,0:T(8,128)} %bitcast.19), custom_call_target="tpu_custom_call" | custom-call | tf_op jit(solution)/shard_map/parareal/pallas_call | solution.py:550
  27.5 0.9 %deliver.1 = (f32[2,64,8,128]{3,2,1,0:T(8,128)}, f32[2,32,128]{2,1,0:T(8,128)}) custom-call(f32[2,8,64,128]{3,2,1,0:T(8,128)S(1)} %get-tuple-element.6.ends, f32[2,32,128]{2,1,0:T(8,128)S(1)} %get-tuple-element.7.following), custom_call_target="tpu_custom_call" | custom-call | tf_op jit(solution)/shard_map/deliver/pallas_call | solution.py:591

commit v5 on v4

--- a/solution.py
+++ b/solution.py
@@ -18,8 +18,8 @@
 LANES = 128
 MESH = pl.DeviceIdType.MESH
 SHARE = 2
-EARLY = 4
 SLOTS = 3
+STARTS = (1, 3, 5)
 AREA = 1.0 / (COARSEN * COARSEN)
 
 
@@ -226,10 +226,9 @@
         ers[1 + f] = jnp.sum(sums[f], axis=0) * AREA
     erg[r] = ers[...]
 
-    def send_rows(first, last):
-        for d in range(first, last + 1):
-            for side in range(2):
-                pl.when(sends[side])(lambda: v_copy(side, d).start())
+    def send_row(d):
+        for side in range(2):
+            pl.when(sends[side])(lambda: v_copy(side, d).start())
 
     def columns_of(i, k):
         right = 0.5 * (k + to_right(k))
@@ -304,12 +303,14 @@
                 ku[i] = edge
                 centre_of(i - 1)
 
-    pass_on(1)
+    for d in range(1, 5):
+        pass_on(d)
     for level in range(1, FINE):
-        pass_on(level + 1)
+        for d in range(2 * level + 3, min(2 * level + 4, FINE) + 1):
+            pass_on(d)
         faces_at(level)
-        if level == 1:
-            send_rows(1, EARLY)
+        if level in STARTS:
+            send_row(STARTS.index(level) + 1)
         if level in (2, 4):
             relay(level // 2)
         if level == 4:
@@ -366,9 +367,6 @@
     def run_diagonal(diagonal):
         for side in range(2):
             pl.when(gets[side])(lambda: v_copy(side, diagonal).wait_recv())
-        if diagonal != 3:
-            send_rows(diagonal + EARLY, min(diagonal + EARLY, FINE))
-
         def step(level, carry):
             row_pair(level, diagonal)
             return carry
@@ -379,7 +377,7 @@
 
     run_diagonal(1)
     run_diagonal(2)
-    send_rows(EARLY + 3, EARLY + 3)
+    send_row(4)
 
     for o in range(1, nr):
         er_copy(o).wait_recv()
@@ -411,6 +409,7 @@
             state = tuple(new)
         return state
 
+    send_row(5)
     later = jnp.where(t > 0, 1.0, 0.0)
     old = coarse_prop(tuple(later * erg[i, 1 + f] for f in range(2) for i in range(nr)))
 
@@ -431,8 +430,11 @@
     for o in range(1, nt):
         pl.when(t + o < nt)(lambda: j_copy(o).start())
 
+    send_row(6)
     for d in range(3, FINE):
         run_diagonal(d)
+        if d < 5:
+            send_row(d + 4)
 
     def place(level, side):
         return level if side == 0 else 3 * SUB - 1 - level

time: 28.6 us -> 28.6 us (level)
  the two profiles are of different devices: /device:TPU:15 before, /device:TPU:0 now
where the time goes in v5:
time: 28.6 us; the launch traced here: 28.2 us
  Pallas kernels  27.6 us (97%)
  between operations  0.64 us (2%)
    pallas_call x1, Pallas kernels, body(): pl.pallas_call(functools.partial(kernel, nt, nr, group), out_shape=(jax.S...  26.6 us
    pallas_call x1, Pallas kernels, body(): pl.pallas_call(deliver, out_shape=(jax.ShapeDtypeStruct((2, blocks, rows,...  0.94 us

profile of v5, /device:TPU:0, one launch (start us, length us, event | category | flops | bytes accessed | tf_op | source)
XLA Modules:
  0.0 28.2 jit_solution(10239579049248652434)
XLA Ops:
  0.6 26.6 %parareal.1 = (f32[2,8,64,128]{3,2,1,0:T(8,128)S(1)}, f32[2,32,128]{2,1,0:T(8,128)S(1)}) custom-call(f32[2,512,128]{2,1,0:T(8,128)} %bitcast.18, f32[512,128]{1,0:T(8,128)} %bitcast.19), custom_call_target="tpu_custom_call" | custom-call | tf_op jit(solution)/shard_map/parareal/pallas_call | solution.py:552
  27.3 0.9 %deliver.1 = (f32[2,64,8,128]{3,2,1,0:T(8,128)}, f32[2,32,128]{2,1,0:T(8,128)}) custom-call(f32[2,8,64,128]{3,2,1,0:T(8,128)S(1)} %get-tuple-element.6.ends, f32[2,32,128]{2,1,0:T(8,128)S(1)} %get-tuple-element.7.following), custom_call_target="tpu_custom_call" | custom-call | tf_op jit(solution)/shard_map/deliver/pallas_call | solution.py:593

commit v6 on v5

--- a/solution.py
+++ b/solution.py
@@ -19,6 +19,7 @@
 MESH = pl.DeviceIdType.MESH
 SHARE = 2
 SLOTS = 3
+LATE = 6
 STARTS = (1, 3, 5)
 AREA = 1.0 / (COARSEN * COARSEN)
 
@@ -376,8 +377,6 @@
     rate = EXCHANGE * (FINE / COARSE)
 
     run_diagonal(1)
-    run_diagonal(2)
-    send_row(4)
 
     for o in range(1, nr):
         er_copy(o).wait_recv()
@@ -409,10 +408,12 @@
             state = tuple(new)
         return state
 
-    send_row(5)
     later = jnp.where(t > 0, 1.0, 0.0)
     old = coarse_prop(tuple(later * erg[i, 1 + f] for f in range(2) for i in range(nr)))
 
+    send_row(4)
+    run_diagonal(2)
+    send_row(5)
     for o in range(1, nr):
         ct_copy(o).wait_recv()
     change = []
@@ -431,19 +432,36 @@
         pl.when(t + o < nt)(lambda: j_copy(o).start())
 
     send_row(6)
-    for d in range(3, FINE):
+    for d in range(3, LATE):
         run_diagonal(d)
         if d < 5:
             send_row(d + 4)
 
-    def place(level, side):
-        return level if side == 0 else 3 * SUB - 1 - level
-
-    for level in range(1, FINE + 1):
+    def place(level, side, d):
+        return SUB + level - d if side == 0 else 2 * SUB - 1 - level + d
+
+    def prepare(d):
+        for level in range(1, FINE + 1):
+            for side in range(2):
+                i = place(level, side, d)
+                for f, x in enumerate(advance(ub, (level - 1) % 2, i, above=side == 1, below=side == 0)):
+                    part[level - 1, side, f] = x
+
+    def complete(d):
         for side in range(2):
-            heat, tracer = advance(ub, (level - 1) % 2, place(level, side), above=side == 1, below=side == 0)
-            part[level - 1, side, 0] = heat
-            part[level - 1, side, 1] = tracer
+            pl.when(gets[side])(lambda: v_copy(side, d).wait_recv())
+        ends = [[ub[0, place(0, side, d), f] for f in range(2)] for side in range(2)]
+        for level in range(1, FINE + 1):
+            for side in range(2):
+                i = place(level, side, d)
+                face = (ku, kd)[side][i]
+                heat, tracer = ends[side]
+                ends[side] = [part[level - 1, side, 0] + face * heat,
+                              part[level - 1, side, 1] + (TRACER_DIFF * face) * tracer]
+                if d < FINE and level < FINE:
+                    for f in range(2):
+                        ub[level % 2, i, f] = ends[side][f]
+        return ends
 
     share = FINE // group
     for side in range(2):
@@ -473,13 +491,27 @@
         pltpu.make_async_remote_copy(
             jall.at[n], jall.at[n], jsend.at[0], jrecv.at[n],
             device_id=(n, r), device_id_type=MESH).wait_recv()
-        state = coarse_prop(state)
-        return tuple(state[f * nr + i] + jall[n, i, f] for f in range(2) for i in range(nr))
+        return coarse_prop(tuple(state[f * nr + i] + jall[n, i, f] for f in range(2) for i in range(nr)))
+
+    def write_row(row, ends):
+        for f in range(2):
+            end = exchange_lanes([ends[f][m] + fix[f] for m in range(COARSEN)])
+            for m in range(SUB):
+                out_ref[f, row, m * SUB:(m + 1) * SUB, :] = end[m]
+
+    def write_pair(d, ends):
+        write_row(FINE - d, ends[0])
+        write_row(d - 1, ends[1])
+
+    prepare(LATE)
+    early = complete(LATE)
+    for side, row in enumerate((FINE - LATE, LATE - 1)):
+        for f in range(2):
+            ub[FINE % 2, SUB + row, f] = early[side][f]
+    prepare(LATE + 1)
 
     state = tuple(jnp.zeros((SUB, LANES), f32) for _ in range(2 * nr))
     state = lax.fori_loop(0, t, link, state)
-    state = coarse_prop(state)
-
     fix = [None, None]
     for f in range(2):
         for i in range(nr):
@@ -491,30 +523,13 @@
             n = f * nr + i
             nxt_ref[f, pl.ds(i, SUB, stride=nr), :] = lines_to_lanes(natural[n * SUB:(n + 1) * SUB])
 
-    def write_row(row, f, end):
-        end = exchange_lanes([end[m] + fix[f] for m in range(COARSEN)])
-        for m in range(SUB):
-            out_ref[f, row, m * SUB:(m + 1) * SUB, :] = end[m]
-
-    for row in range(1, SUB - 1):
-        for f in range(2):
-            write_row(row, f, ub[0, SUB + row, f])
-
-    last = []
-    for side in range(2):
-        pl.when(gets[side])(lambda: v_copy(side, FINE).wait_recv())
-    for side in range(2):
-        i = place(0, side)
-        last.append([ub[0, i, 0], ub[0, i, 1]])
-    for level in range(1, FINE + 1):
-        for side in range(2):
-            face = (ku, kd)[side][place(level, side)]
-            heat, tracer = last[side]
-            last[side] = [part[level - 1, side, 0] + face * heat,
-                          part[level - 1, side, 1] + (TRACER_DIFF * face) * tracer]
-    for side in range(2):
-        for f in range(2):
-            write_row((0, SUB - 1)[side], f, last[side][f])
+    for row in range(FINE - LATE, LATE):
+        write_row(row, [ub[FINE % 2, SUB + row, f] for f in range(2)])
+    for d in range(LATE + 1, FINE + 1):
+        ends = complete(d)
+        if d < FINE:
+            prepare(d + 1)
+        write_pair(d, ends)
 
     for side in range(2):
         @pl.when(sends[side])

time: 28.6 us -> 27 us (0.944); the launches traced: 28.2 us -> 26.9 us
  Pallas kernels: 27.6 us -> 26.2 us
    pallas_call x1, Pallas kernels: 26.6 us -> 25.3 us  [body(): pl.pallas_call(functools.partial(kernel, nt, nr, group), out_shape=(jax.S...]
where the time goes in v6:
time: 27 us; the launch traced here: 26.9 us
  Pallas kernels  26.2 us (97%)
  between operations  0.64 us (2%)
    pallas_call x1, Pallas kernels, body(): pl.pallas_call(functools.partial(kernel, nt, nr, group), out_shape=(jax.S...  25.3 us
    pallas_call x1, Pallas kernels, body(): pl.pallas_call(deliver, out_shape=(jax.ShapeDtypeStruct((2, blocks, rows,...  0.94 us

profile of v6, /device:TPU:0, one launch (start us, length us, event | category | flops | bytes accessed | tf_op | source)
XLA Modules:
  0.0 26.9 jit_solution(2890935684731200082)
XLA Ops:
  0.6 25.3 %parareal.1 = (f32[2,8,64,128]{3,2,1,0:T(8,128)S(1)}, f32[2,32,128]{2,1,0:T(8,128)S(1)}) custom-call(f32[2,512,128]{2,1,0:T(8,128)} %bitcast.18, f32[512,128]{1,0:T(8,128)} %bitcast.19), custom_call_target="tpu_custom_call" | custom-call | tf_op jit(solution)/shard_map/parareal/pallas_call | solution.py:567
  25.9 0.9 %deliver.1 = (f32[2,64,8,128]{3,2,1,0:T(8,128)}, f32[2,32,128]{2,1,0:T(8,128)}) custom-call(f32[2,8,64,128]{3,2,1,0:T(8,128)S(1)} %get-tuple-element.6.ends, f32[2,32,128]{2,1,0:T(8,128)S(1)} %get-tuple-element.7.following), custom_call_target="tpu_custom_call" | custom-call | tf_op jit(solution)/shard_map/deliver/pallas_call | solution.py:608

commit v7 on v6

--- a/solution.py
+++ b/solution.py
@@ -141,26 +141,8 @@
         return jnp.stack(exchange_lanes(
             [ref[pl.ds(m * SUB * SUB + row, SUB, stride=SUB), :] for m in range(SUB)]), axis=0)
 
-    k_in.wait()
-    total = None
-    for row in outer_first:
-        x = read_row(k_ref, row)
-        kown[row] = x
-        total = x if total is None else total + x
-    ers[0] = jnp.sum(total, axis=0) * AREA
-
-    pl.semaphore_wait(barrier, t + (group - 1 - member) + has_up.astype(jnp.int32) + has_down.astype(jnp.int32))
-
     def tell(tok, row):
         pl.semaphore_signal(tok, inc=1, device_id=(t, row), device_id_type=MESH)
-
-    pl.when(jnp.logical_not(has_up) & has_down)(lambda: tell(tok_down, r + 1))
-    pl.when(jnp.logical_not(has_down) & has_up)(lambda: tell(tok_up, r - 1))
-
-    for o in range(1, nt):
-        @pl.when(t >= o)
-        def _():
-            pl.semaphore_signal(tok_tm, inc=1, device_id=(t - o, r), device_id_type=MESH)
 
     def relay(slot):
         @pl.when(has_up & (jnp.minimum(r - 1, SLOTS - 1) == slot))
@@ -176,43 +158,82 @@
     def v_copy(side, d):
         if side == 0:
             return pltpu.make_async_remote_copy(
-                own.at[SUB - d], ub.at[0, SUB - d], vsend.at[side], vrecv.at[side, d - 1],
+                own.at[SUB - d], ub.at[0, SUB - d], vsend.at[side], vrecv.at[d - 1],
                 device_id=(t, r + 1), device_id_type=MESH)
         return pltpu.make_async_remote_copy(
-            own.at[d - 1], ub.at[0, 2 * SUB - 1 + d], vsend.at[side], vrecv.at[side, d - 1],
+            own.at[d - 1], ub.at[0, 2 * SUB - 1 + d], vsend.at[side], vrecv.at[d - 1],
             device_id=(t, r - 1), device_id_type=MESH)
 
     def k_copy(side, d):
         return pltpu.make_async_remote_copy(
-            kown.at[SUB - d if side == 0 else d - 1], kh.at[side, d - 1], ksend.at[side], krecv.at[side, d - 1],
+            kown.at[SUB - d if side == 0 else d - 1], kh.at[side, d - 1], ksend.at[side], krecv.at[d - 1],
             device_id=(t, r + 1 if side == 0 else r - 1), device_id_type=MESH)
 
     def k_forward(side, d, o):
         return pltpu.make_async_remote_copy(
-            kh.at[side, d - 1], kh.at[side, d - 1], kfwd.at[side], krecv.at[side, d - 1],
+            kh.at[side, d - 1], kh.at[side, d - 1], kfwd.at[side], krecv.at[d - 1],
             device_id=(base + lax.rem(member + o, group), r), device_id_type=MESH)
+
+    def both_sides(array, sem):
+        for count, cond in ((2, has_up & has_down), (1, jnp.logical_xor(has_up, has_down))):
+            @pl.when(cond)
+            def _():
+                rows = array.at[pl.ds(0, count)]
+                pltpu.make_async_remote_copy(
+                    rows, rows, ksend.at[0], sem, device_id=(t, jnp.where(has_up, r - 1, r + 1)), device_id_type=MESH).wait_recv()
 
     def mine(d):
         return member == (d - 1) % group
 
     def er_copy(o):
         return pltpu.make_async_remote_copy(
-            ers, erg.at[r], ersend, errecv.at[o],
+            ers, erg.at[r], ersend, errecv,
             device_id=(t, lax.rem(r + o, nr)), device_id_type=MESH)
 
-    def ct_copy(o):
-        return pltpu.make_async_remote_copy(
-            cts, ctg.at[r], ctsend, ctrecv.at[o],
+    at_edge = jnp.logical_not(has_up & has_down)
+    skipped = jnp.where(has_up, 0, 1)
+
+    def ct_rows(count, o):
+        first = skipped if count == 2 else 0
+        return pltpu.make_async_remote_copy(
+            cts.at[pl.ds(first, count)], ctg.at[pl.ds(3 * r + first, count)], ctsend, ctrecv,
             device_id=(t, lax.rem(r + o, nr)), device_id_type=MESH)
+
+    def ct_total(count):
+        rows = ctg.at[pl.ds(0, count)]
+        return pltpu.make_async_remote_copy(
+            rows, rows, ctsend, ctrecv, device_id=(t, lax.rem(r + 1, nr)), device_id_type=MESH)
 
     def j_copy(o):
         return pltpu.make_async_remote_copy(
             jall.at[t], jall.at[t], jsend.at[o], jrecv.at[t],
             device_id=(t + o, r), device_id_type=MESH)
 
-    for d in range(1, FINE + 1):
+    def send_conductivity(d):
         for side in range(2):
             pl.when(sends[side] & mine(d))(lambda: k_copy(side, d).start())
+
+    k_in.wait()
+    total = None
+    for d in range(1, SUB // 2 + 1):
+        for row in (SUB - d, d - 1):
+            x = read_row(k_ref, row)
+            kown[row] = x
+            total = x if total is None else total + x
+        if d == 1:
+            pl.semaphore_wait(barrier, t + (group - 1 - member) + has_up.astype(jnp.int32) + has_down.astype(jnp.int32))
+
+            pl.when(jnp.logical_not(has_up) & has_down)(lambda: tell(tok_down, r + 1))
+            pl.when(jnp.logical_not(has_down) & has_up)(lambda: tell(tok_up, r - 1))
+
+            for o in range(1, nt):
+                @pl.when(t >= o)
+                def _():
+                    pl.semaphore_signal(tok_tm, inc=1, device_id=(t - o, r), device_id_type=MESH)
+        send_conductivity(d)
+    for d in range(SUB // 2 + 1, FINE + 1):
+        send_conductivity(d)
+    ers[0] = jnp.sum(total, axis=0) * AREA
 
     s_in.wait()
     sums = [None, None]
@@ -277,18 +298,22 @@
                 ub[1 - p, SUB + row, f] = x
 
     def pass_on(d):
+        @pl.when(mine(d))
+        def _():
+            both_sides(kown, krecv.at[d - 1])
         for side in range(2):
             @pl.when(gets[side] & mine(d))
             def _():
-                k_copy(side, d).wait_recv()
                 for o in range(1, group):
                     k_forward(side, d, o).start()
 
     outside = (jnp.where(has_up, 1.0, 0.0), jnp.where(has_down, 1.0, 0.0))
 
     def faces_at(d):
+        @pl.when(jnp.logical_not(mine(d)))
+        def _():
+            both_sides(kown, krecv.at[d - 1])
         for side in range(2):
-            pl.when(gets[side] & jnp.logical_not(mine(d)))(lambda: k_copy(side, d).wait_recv())
             k = kh[side, d - 1]
             inner = kh[side, d - 2] if d > 1 else kown[0 if side == 0 else SUB - 1]
             face = 0.5 * (k + inner)
@@ -304,17 +329,18 @@
                 ku[i] = edge
                 centre_of(i - 1)
 
+    send_row(1)
     for d in range(1, 5):
         pass_on(d)
+    relay(1)
     for level in range(1, FINE):
         for d in range(2 * level + 3, min(2 * level + 4, FINE) + 1):
             pass_on(d)
         faces_at(level)
         if level in STARTS:
-            send_row(STARTS.index(level) + 1)
-        if level in (2, 4):
-            relay(level // 2)
+            send_row(STARTS.index(level) + 2)
         if level == 4:
+            relay(2)
             for o in range(1, nr):
                 er_copy(o).start()
         p = (level - 1) % 2
@@ -354,8 +380,9 @@
         cts[b, 0] = AREA * ((whole[0] + moved) + gain[0])
         cts[b, 1] = AREA * ((whole[1] - moved) + gain[1])
     for o in range(1, nr):
-        ct_copy(o).start()
-    ctg[r] = cts[...]
+        pl.when(at_edge)(lambda: ct_rows(2, o).start())
+        pl.when(jnp.logical_not(at_edge))(lambda: ct_rows(3, o).start())
+    ctg[pl.ds(3 * r, 3)] = cts[...]
     faces_at(FINE)
 
     def row_pair(level, diagonal):
@@ -366,8 +393,7 @@
             ub[1 - p, i, 1] = tracer
 
     def run_diagonal(diagonal):
-        for side in range(2):
-            pl.when(gets[side])(lambda: v_copy(side, diagonal).wait_recv())
+        both_sides(own, vrecv.at[diagonal - 1])
         def step(level, carry):
             row_pair(level, diagonal)
             return carry
@@ -378,8 +404,12 @@
 
     run_diagonal(1)
 
-    for o in range(1, nr):
-        er_copy(o).wait_recv()
+    def er_total():
+        rows = erg.at[pl.ds(0, nr - 1)]
+        return pltpu.make_async_remote_copy(
+            rows, rows, ersend, errecv, device_id=(t, lax.rem(r + 1, nr)), device_id_type=MESH)
+
+    er_total().wait_recv()
     kcv = [erg[i, 0] for i in range(nr)]
     c_right = [ratio * 0.5 * (k + following(k)) for k in kcv]
     c_left = [ratio * 0.5 * (k + preceding(k)) for k in kcv]
@@ -411,19 +441,19 @@
     later = jnp.where(t > 0, 1.0, 0.0)
     old = coarse_prop(tuple(later * erg[i, 1 + f] for f in range(2) for i in range(nr)))
 
-    send_row(4)
+    send_row(5)
     run_diagonal(2)
-    send_row(5)
-    for o in range(1, nr):
-        ct_copy(o).wait_recv()
+    send_row(6)
+    pl.when(at_edge)(lambda: ct_total(3 * nr - 4).wait_recv())
+    pl.when(jnp.logical_not(at_edge))(lambda: ct_total(3 * nr - 5).wait_recv())
     change = []
     for f in range(2):
         for i in range(nr):
-            x = ctg[i, 1, f]
+            x = ctg[3 * i + 1, f]
             if i > 0:
-                x = x + ctg[i - 1, 2, f]
+                x = x + ctg[3 * i - 1, f]
             if i < nr - 1:
-                x = x + ctg[i + 1, 0, f]
+                x = x + ctg[3 * i + 3, f]
             x = x - old[f * nr + i]
             jall[t, i, f] = x
             change.append(x)
@@ -431,11 +461,11 @@
     for o in range(1, nt):
         pl.when(t + o < nt)(lambda: j_copy(o).start())
 
-    send_row(6)
+    send_row(7)
     for d in range(3, LATE):
         run_diagonal(d)
-        if d < 5:
-            send_row(d + 4)
+        if d == 3:
+            send_row(8)
 
     def place(level, side, d):
         return SUB + level - d if side == 0 else 2 * SUB - 1 - level + d
@@ -448,8 +478,7 @@
                     part[level - 1, side, f] = x
 
     def complete(d):
-        for side in range(2):
-            pl.when(gets[side])(lambda: v_copy(side, d).wait_recv())
+        both_sides(own, vrecv.at[d - 1])
         ends = [[ub[0, place(0, side, d), f] for f in range(2)] for side in range(2)]
         for level in range(1, FINE + 1):
             for side in range(2):
@@ -468,7 +497,7 @@
         @pl.when(sends[side])
         def _():
             pltpu.make_async_remote_copy(
-                kown.at[pl.ds(0, share)], kh.at[side, pl.ds(0, share)], ksend.at[side], krecv.at[side, 0],
+                kown.at[pl.ds(0, share)], kh.at[side, pl.ds(0, share)], ksend.at[side], krecv.at[0],
                 device_id=(t, r + 1 if side == 0 else r - 1), device_id_type=MESH).wait_send()
 
         if group > 1:
@@ -476,14 +505,11 @@
             def _():
                 passed = kh.at[side, pl.ds(0, share * (group - 1))]
                 pltpu.make_async_remote_copy(
-                    passed, passed, kfwd.at[side], krecv.at[side, 0],
+                    passed, passed, kfwd.at[side], krecv.at[0],
                     device_id=(base + lax.rem(member + 1, group), r), device_id_type=MESH).wait_send()
-    if nr > 1:
-        for ref, send, recv in ((erg, ersend, errecv), (ctg, ctsend, ctrecv)):
-            spread = ref.at[pl.ds(0, nr - 1)]
-            pltpu.make_async_remote_copy(
-                spread, spread, send, recv.at[0],
-                device_id=(t, lax.rem(r + 1, nr)), device_id_type=MESH).wait_send()
+    er_total().wait_send()
+    pl.when(at_edge)(lambda: ct_total(2 * nr - 2).wait_send())
+    pl.when(jnp.logical_not(at_edge))(lambda: ct_total(3 * nr - 3).wait_send())
     for o in range(1, nt):
         pl.when(t + o < nt)(lambda: j_copy(o).wait_send())
 
@@ -535,7 +561,7 @@
         @pl.when(sends[side])
         def _():
             pltpu.make_async_remote_copy(
-                own, ub.at[0, pl.ds(0, SUB)], vsend.at[side], vrecv.at[side, 0],
+                own, ub.at[0, pl.ds(0, SUB)], vsend.at[side], vrecv.at[0],
                 device_id=(t, r + 1 if side == 0 else r - 1), device_id_type=MESH).wait_send()
 
 
@@ -553,6 +579,7 @@
 def body(nt, nr, starts, conductivity):
     rows, columns = conductivity.shape
     assert rows == SUB == COARSEN == FINE
+    assert nr > 1
     assert columns == COARSEN * SUB * LANES
     blocks = columns // LANES
     group = math.gcd(SHARE, nt)
@@ -592,12 +619,11 @@
             pltpu.VMEM((3,) + cell, f32),
             pltpu.VMEM((nr, 3) + cell, f32),
             pltpu.VMEM((3, 2) + cell, f32),
-            pltpu.VMEM((nr, 3, 2) + cell, f32),
+            pltpu.VMEM((3 * nr, 2) + cell, f32),
             pltpu.VMEM((nt, nr, 2) + cell, f32),
-            dma((2,)), dma((2, FINE)),
-            dma((2,)), dma((2, FINE)), dma((2,)),
-            dma, dma((nr,)),
-            dma, dma((nr,)),
+            dma((2,)), dma((FINE,)),
+            dma((2,)), dma((FINE,)), dma((2,)),
+            dma, dma, dma, dma,
             dma((nt,)), dma((nt,)),
             pltpu.SemaphoreType.REGULAR, pltpu.SemaphoreType.REGULAR, pltpu.SemaphoreType.REGULAR,
         ],

time: 27 us -> 25.7 us (0.952)
  Pallas kernels: 26.2 us -> 24.7 us
    pallas_call x1, Pallas kernels: 25.3 us -> 23.8 us  [body(): pl.pallas_call(functools.partial(kernel, nt, nr, group), out_shape=(jax.S...]
where the time goes in v7:
time: 25.7 us; the launch traced here: 25.4 us
  Pallas kernels  24.7 us (96%)
  between operations  0.64 us (2%)
    pallas_call x1, Pallas kernels, body(): pl.pallas_call(functools.partial(kernel, nt, nr, group), out_shape=(jax.S...  23.8 us
    pallas_call x1, Pallas kernels, body(): pl.pallas_call(deliver, out_shape=(jax.ShapeDtypeStruct((2, blocks, rows,...  0.94 us

profile of v7, /device:TPU:0, one launch (start us, length us, event | category | flops | bytes accessed | tf_op | source)
XLA Modules:
  0.0 25.4 jit_solution(8025574543739815930)
XLA Ops:
  0.6 23.8 %parareal.1 = (f32[2,8,64,128]{3,2,1,0:T(8,128)S(1)}, f32[2,32,128]{2,1,0:T(8,128)S(1)}) custom-call(f32[2,512,128]{2,1,0:T(8,128)} %bitcast.18, f32[512,128]{1,0:T(8,128)} %bitcast.19), custom_call_target="tpu_custom_call" | custom-call | tf_op jit(solution)/shard_map/parareal/pallas_call | solution.py:594
  24.4 0.9 %deliver.1 = (f32[2,64,8,128]{3,2,1,0:T(8,128)}, f32[2,32,128]{2,1,0:T(8,128)}) custom-call(f32[2,8,64,128]{3,2,1,0:T(8,128)S(1)} %get-tuple-element.6.ends, f32[2,32,128]{2,1,0:T(8,128)S(1)} %get-tuple-element.7.following), custom_call_target="tpu_custom_call" | custom-call | tf_op jit(solution)/shard_map/deliver/pallas_call | solution.py:634

commit v8 on v7

--- a/solution.py
+++ b/solution.py
@@ -20,7 +20,7 @@
 SHARE = 2
 SLOTS = 3
 LATE = 6
-STARTS = (1, 3, 5)
+STARTS = (1, 4)
 AREA = 1.0 / (COARSEN * COARSEN)
 
 
@@ -339,7 +339,7 @@
         faces_at(level)
         if level in STARTS:
             send_row(STARTS.index(level) + 2)
-        if level == 4:
+        if level == 3:
             relay(2)
             for o in range(1, nr):
                 er_copy(o).start()
@@ -403,6 +403,9 @@
     rate = EXCHANGE * (FINE / COARSE)
 
     run_diagonal(1)
+    send_row(4)
+    run_diagonal(2)
+    send_row(5)
 
     def er_total():
         rows = erg.at[pl.ds(0, nr - 1)]
@@ -441,8 +444,7 @@
     later = jnp.where(t > 0, 1.0, 0.0)
     old = coarse_prop(tuple(later * erg[i, 1 + f] for f in range(2) for i in range(nr)))
 
-    send_row(5)
-    run_diagonal(2)
+    run_diagonal(3)
     send_row(6)
     pl.when(at_edge)(lambda: ct_total(3 * nr - 4).wait_recv())
     pl.when(jnp.logical_not(at_edge))(lambda: ct_total(3 * nr - 5).wait_recv())
@@ -462,9 +464,9 @@
         pl.when(t + o < nt)(lambda: j_copy(o).start())
 
     send_row(7)
-    for d in range(3, LATE):
+    for d in range(4, LATE):
         run_diagonal(d)
-        if d == 3:
+        if d == 4:
             send_row(8)
 
     def place(level, side, d):

time: 25.7 us -> 25.3 us (0.984)
  no operation moved by 1% of the time
where the time goes in v8:
time: 25.3 us; the launch traced here: 25.1 us
  Pallas kernels  24.5 us (97%)
  between operations  0.64 us (3%)
    pallas_call x1, Pallas kernels, body(): pl.pallas_call(functools.partial(kernel, nt, nr, group), out_shape=(jax.S...  23.6 us
    pallas_call x1, Pallas kernels, body(): pl.pallas_call(deliver, out_shape=(jax.ShapeDtypeStruct((2, blocks, rows,...  0.94 us

profile of v8, /device:TPU:0, one launch (start us, length us, event | category | flops | bytes accessed | tf_op | source)
XLA Modules:
  0.0 25.1 jit_solution(10239579621275879345)
XLA Ops:
  0.6 23.6 %parareal.1 = (f32[2,8,64,128]{3,2,1,0:T(8,128)S(1)}, f32[2,32,128]{2,1,0:T(8,128)S(1)}) custom-call(f32[2,512,128]{2,1,0:T(8,128)} %bitcast.18, f32[512,128]{1,0:T(8,128)} %bitcast.19), custom_call_target="tpu_custom_call" | custom-call | tf_op jit(solution)/shard_map/parareal/pallas_call | solution.py:596
  24.2 0.9 %deliver.1 = (f32[2,64,8,128]{3,2,1,0:T(8,128)}, f32[2,32,128]{2,1,0:T(8,128)}) custom-call(f32[2,8,64,128]{3,2,1,0:T(8,128)S(1)} %get-tuple-element.6.ends, f32[2,32,128]{2,1,0:T(8,128)S(1)} %get-tuple-element.7.following), custom_call_target="tpu_custom_call" | custom-call | tf_op jit(solution)/shard_map/deliver/pallas_call | solution.py:636
